TPU v7x, 32 devices: a whole 2x2x4 slice. The times are simulated.
32 devices in a mesh: groups: 2 (over x), expert: 16 (over z, y, core).
Axes of the slice: x: 2, y: 2, z: 4, core: 2. Of those that a mesh axis runs over, the one named last changes fastest.
Arguments:
- residual: bfloat16 [4096, 3584], P(('groups', 'expert')), parts along dimension 0, may hold values from -24 to 24
- norm_gain: float32 [3584], replicated, may hold values from 0.25 to 1.75
- router: bfloat16 [3584, 4], replicated, may hold values from -0.09375 to 0.09375
- w_gate: bfloat16 [3584, 4096], P(None, 'expert'), may hold values from -0.09375 to 0.09375
- w_up: bfloat16 [3584, 4096], P(None, 'expert'), may hold values from -0.09375 to 0.09375
- w_down: bfloat16 [4096, 3584], P('expert'), may hold values from -0.1875 to 0.1875
- expert_ids: int32 [4096, 2], P(('groups', 'expert')), parts along dimension 0, may hold values from 0 to 3, all different within a row; in each aligned block of 128 rows (0 to 127, 128 to 255, ...) at most 96 rows name the same one
Outputs:
- layer_out: bfloat16 [4096, 3584], P(('groups', 'expert')), parts along dimension 0
There are 2 independent parts, one for each index of `groups`. A program takes and returns all parts, laid end to end along the dimension named above; an argument that names none is the same for every part. Nothing has to cross between parts.
Inputs may be any that keep to these rules, and one draw needn't show every extreme that they name: `expert_ids`: each row names 2 different experts. Within the rows of one device no expert is named by more than 96 rows, and in every draw some device's rows name some expert exactly 96 times.
All inputs are finite; a program needn't handle non-finite values.
Results may differ from a plain program's by a relative error of at most 0.0054.
Values may be sent and summed in bfloat16 or wider, within the bound.
A program may use at most 128 MiB of HBM per device.

v0:
```python
import functools

import jax
import jax.numpy as jnp
from jax import lax
from jax.experimental import pallas as pl
from jax.experimental.pallas import tpu as pltpu
from jax.sharding import PartitionSpec as P

route_scale = 2.5
norm_eps = 1e-06
LANES = 128
MESH = pl.DeviceIdType.MESH

TOK_PIECES = 2
OUT_PIECES = 7
W_PIECES = (4, 4, 7)


def kernel(
    groups,
    experts,
    span,
    capacity,
    res_ref,
    gain_ref,
    router_ref,
    ids_ref,
    wg_in,
    wu_in,
    wd_in,
    out_ref,
    tok,
    gates,
    act,
    rx,
    acc,
    wg,
    wu,
    wd,
    own_sem,
    tok_recv,
    tok_up,
    tok_dn,
    gate_recv,
    gate_up,
    gate_dn,
    ret_send,
    ret_recv,
    y_send,
    y_recv,
    x_send,
    x_recv,
    c_send,
    c_recv,
    cy_send,
    cy_recv,
    cx_send,
    cx_recv,
):
    rows, width = res_ref.shape
    hid = wg_in.shape[1]
    grp = lax.axis_index("groups")
    pos = lax.axis_index("expert")
    exp = pos // span
    mem = pos % span
    last = experts - 1
    has_up = exp < last
    has_dn = exp > 0
    base = exp * span
    mem_y = (mem + 2) % 4
    mem_c = mem + 1 - 2 * (mem % 2)
    mem_yc = (mem_c + 2) % 4
    up = {"groups": grp, "expert": jnp.minimum(pos + span, experts * span - 1)}
    dn = {"groups": grp, "expert": jnp.maximum(pos - span, 0)}
    to_y = {"groups": grp, "expert": base + mem_y}
    to_c = {"groups": grp, "expert": base + mem_c}

    def other(i):
        return (grp + 1 + i) % groups

    barrier = pltpu.get_barrier_semaphore()

    def greet(device):
        pl.semaphore_signal(barrier, inc=1, device_id=device, device_id_type=MESH)

    greet(to_y)
    greet(to_c)
    for i in range(groups - 1):
        greet({"groups": other(i), "expert": pos})

    @pl.when(has_up)
    def _():
        greet(up)

    @pl.when(has_dn)
    def _():
        greet(dn)

    peers = 1 + groups + has_up.astype(jnp.int32) + has_dn.astype(jnp.int32)
    pl.semaphore_wait(barrier, peers)

    mats = ((wg_in, wg), (wu_in, wu), (wd_in, wd))

    def piece(ref, mat, group, index):
        total = mats[mat][0].shape[mat // 2]
        size = total // groups // W_PIECES[mat]
        part = pl.ds(pl.multiple_of(group * (total // groups) + index * size, size), size)
        return ref.at[:, part] if mat == 2 else ref.at[part]

    def number(mat, index):
        return sum(W_PIECES[:mat]) + index

    def remote(src, dst, send, recv, device):
        return pltpu.make_async_remote_copy(
            src_ref=src, dst_ref=dst, send_sem=send, recv_sem=recv, device_id=device, device_id_type=MESH
        )

    def y_copy(mat, index, landing):
        at = number(mat, index)
        into = piece(mats[mat][1].at[mem_y if landing else mem], mat, grp, index)
        return remote(piece(mats[mat][0], mat, grp, index), into, y_send.at[at], y_recv.at[at], to_y)

    def x_copy(mat, index, i, landing):
        at = number(mat, index)
        group = (grp + groups - 1 - i) % groups if landing else grp
        ref = piece(mats[mat][1].at[mem_y], mat, group, index)
        return remote(ref, ref, x_send.at[i, at], x_recv.at[i, at], {"groups": other(i), "expert": pos})

    def cy_copy(mat, index, landing):
        at = number(mat, index)
        ref = piece(mats[mat][1].at[mem_yc if landing else mem_y], mat, grp, index)
        return remote(ref, ref, cy_send.at[at], cy_recv.at[at], to_c)

    def cx_copy(mat, index, i, landing):
        at = number(mat, index)
        group = (grp + groups - 1 - i) % groups
        ref = piece(mats[mat][1].at[mem_yc if landing else mem_y], mat, group, index)
        return remote(ref, ref, cx_send.at[i, at], cx_recv.at[i, at], to_c)

    def c_copy(mat, landing):
        slot = mem_c if landing else mem
        return remote(mats[mat][0], mats[mat][1].at[slot], c_send.at[mat], c_recv.at[mat], to_c)

    for mat in range(3):
        for index in range(W_PIECES[mat]):
            y_copy(mat, index, False).start()
    own_copies = [pltpu.make_async_copy(mats[i][0], mats[i][1].at[mem], own_sem.at[i]) for i in range(3)]
    for mat in range(3):
        c_copy(mat, False).start()
        own_copies[mat].start()

    step_rows = 16

    def norm_rows(i, carry):
        at = pl.ds(pl.multiple_of(i * step_rows, step_rows), step_rows)
        wide = res_ref[at, :].astype(jnp.float32)
        mean = jnp.mean(wide * wide, axis=1, keepdims=True)
        tok[exp, at, :] = (wide * lax.rsqrt(mean + norm_eps) * gain_ref[...].reshape(1, width)).astype(jnp.bfloat16)
        return carry

    piece_rows = rows // TOK_PIECES

    def tok_copy(block, index, upward):
        ref = tok.at[block, pl.ds(index * piece_rows, piece_rows)]
        send = (tok_up if upward else tok_dn).at[block, index]
        return remote(ref, ref, send, tok_recv.at[block, index], up if upward else dn)

    def gate_copy(block, upward):
        ref = gates.at[block]
        send = (gate_up if upward else gate_dn).at[block]
        return remote(ref, ref, send, gate_recv.at[block], up if upward else dn)

    def send_block(block, index, upward):
        tok_copy(block, index, upward).start()
        if index == TOK_PIECES - 1:
            gate_copy(block, upward).start()

    def gate_values():
        logits = lax.dot_general(
            router_ref[...], tok[exp], (((1,), (1,)), ((), ())), preferred_element_type=jnp.float32
        )
        affinity = jax.nn.sigmoid(logits)
        expert = lax.broadcasted_iota(jnp.int32, (experts, rows), 0)
        spread = jnp.zeros((experts, rows), jnp.float32)
        for k in range(ids_ref.shape[0]):
            spread = spread + jnp.where(expert == ids_ref[k : k + 1, :], affinity, 0.0)
        gates[exp] = route_scale * spread / jnp.sum(spread, axis=0, keepdims=True)

    steps = piece_rows // step_rows
    for index in range(TOK_PIECES):
        lax.fori_loop(index * steps, (index + 1) * steps, norm_rows, 0)

        @pl.when(has_up)
        def _():
            tok_copy(exp, index, True).start()

        @pl.when(has_dn)
        def _():
            tok_copy(exp, index, False).start()

    gate_values()

    @pl.when(has_up)
    def _():
        gate_copy(exp, True).start()

    @pl.when(has_dn)
    def _():
        gate_copy(exp, False).start()

    def weight_tick(mat, index):
        y_copy(mat, index, True).wait_recv()
        for i in range(groups - 1):
            x_copy(mat, index, i, False).start()
        cy_copy(mat, index, False).start()

    def weight_late(mat, index):
        for i in range(groups - 1):
            x_copy(mat, index, i, True).wait_recv()
            cx_copy(mat, index, i, False).start()

    def token_tick(step, index):
        low = exp - step
        high = exp + step

        @pl.when(low >= 0)
        def _():
            tok_copy(jnp.maximum(low, 0), index, True).wait_recv()
            if index == TOK_PIECES - 1:
                gate_copy(jnp.maximum(low, 0), True).wait_recv()

        @pl.when(jnp.logical_and(low >= 0, has_up))
        def _():
            send_block(jnp.maximum(low, 0), index, True)

        @pl.when(high <= last)
        def _():
            tok_copy(jnp.minimum(high, last), index, False).wait_recv()
            if index == TOK_PIECES - 1:
                gate_copy(jnp.minimum(high, last), False).wait_recv()

        @pl.when(jnp.logical_and(high <= last, has_dn))
        def _():
            send_block(jnp.minimum(high, last), index, False)

    def hidden_part(block, slot):
        rows_in = tok[block]
        gate_proj = jnp.dot(rows_in, wg[slot], preferred_element_type=jnp.float32)
        up_proj = jnp.dot(rows_in, wu[slot], preferred_element_type=jnp.float32)
        sublane = lax.broadcasted_iota(jnp.int32, (gates.shape[1], rows), 0)
        row = jnp.sum(jnp.where(sublane == exp, gates[block], 0.0), axis=0, keepdims=True)
        scale = jnp.broadcast_to(row, (LANES, rows)).T[:, :1]
        hidden = gate_proj / (1.0 + jnp.exp(-gate_proj)) * up_proj * scale
        act[slot, block] = hidden.astype(jnp.bfloat16)

    def first_slices():
        for mat in range(2):
            own_copies[mat].wait()
            c_copy(mat, True).wait_recv()

    def all_slices():
        for mat in range(2):
            for index in range(W_PIECES[mat]):
                cy_copy(mat, index, True).wait_recv()
                for i in range(groups - 1):
                    cx_copy(mat, index, i, True).wait_recv()

    def hidden_step(step, first, second, count=2):
        def body(i, carry):
            side = i // count
            turn = i % count
            block = exp - step + 2 * step * side
            slot = jnp.where(turn == 0, first, jnp.where(turn == 1, second, jnp.where(turn == 2, mem_y, mem_yc)))

            @pl.when(jnp.logical_and(block >= 0, block <= last))
            def _():
                hidden_part(jnp.clip(block, 0, last), slot)

            return carry

        lax.fori_loop(0, count if step == 0 else 2 * count, body, 0)

    events = []
    for mat in range(3):
        for index in range(W_PIECES[mat]):
            size = 1 / 3 / W_PIECES[mat]
            when = mat / 3 + (index + 1) * size
            events.append((when, 0, functools.partial(weight_tick, mat, index)))
            events.append((when + size, 1, functools.partial(weight_late, mat, index)))
    token_steps = last * TOK_PIECES
    for tick in range(token_steps):
        step, index = divmod(tick, TOK_PIECES)
        events.append(((tick + 1) / token_steps, 2, functools.partial(token_tick, step + 1, index)))
    ready = 0.83
    events.append((0.12, 3, first_slices))
    events.append((ready, 3, all_slices))
    for step in range(experts):
        there = max(step / last, 0.12)
        if there >= ready:
            events.append((there, 4, functools.partial(hidden_step, step, mem, mem_c, span)))
        else:
            events.append((there, 4, functools.partial(hidden_step, step, mem, mem_c)))
            late = ready + 0.04 * step
            events.append((late, 4, functools.partial(hidden_step, step, mem_y, mem_yc)))
    events.sort(key=lambda event: event[:2])
    for event in events:
        event[2]()

    own_copies[2].wait()
    c_copy(2, True).wait_recv()
    for index in range(W_PIECES[2]):
        cy_copy(2, index, True).wait_recv()
        for i in range(groups - 1):
            cx_copy(2, index, i, True).wait_recv()

    def sent(block, carry):
        @pl.when(jnp.logical_and(block <= exp, has_up))
        def _():
            for index in range(TOK_PIECES):
                tok_copy(block, index, True).wait_send()
            gate_copy(block, True).wait_send()

        @pl.when(jnp.logical_and(block >= exp, has_dn))
        def _():
            for index in range(TOK_PIECES):
                tok_copy(block, index, False).wait_send()
            gate_copy(block, False).wait_send()

        return carry

    lax.fori_loop(0, experts, sent, 0)

    cols = width // OUT_PIECES
    tile = 256

    def out_copy(block, index, upward, landing, packed):
        part = pl.ds(index * cols, cols)
        height = pl.ds(0, capacity if packed else rows)
        into = block
        if not upward:
            target = exp if landing else exp - 1
            into = jnp.where(block == target, experts, block)
        return remote(
            tok.at[block, height, part],
            rx.at[into, height, part],
            ret_send.at[block, index],
            ret_recv.at[into, index],
            up if upward else dn,
        )

    def share(block, at, height=rows):
        part = pl.ds(0, height)
        total = jnp.dot(act[0, block, part], wd[0, :, at], preferred_element_type=jnp.float32)
        for slot in range(1, span):
            total = total + jnp.dot(act[slot, block, part], wd[slot, :, at], preferred_element_type=jnp.float32)
        return total

    def packing(block, expert):
        sublane = lax.broadcasted_iota(jnp.int32, (gates.shape[1], rows), 0)
        row = jnp.sum(jnp.where(sublane == expert, gates[block], 0.0), axis=0, keepdims=True)
        taken = jnp.broadcast_to(jnp.where(row != 0.0, 1.0, 0.0), (capacity, rows))
        source = lax.broadcasted_iota(jnp.int32, (rows, rows), 0)
        dest = lax.broadcasted_iota(jnp.int32, (rows, rows), 1)
        earlier = jnp.where(source < dest, 1.0, 0.0).astype(jnp.bfloat16)
        rank = jnp.dot(taken.astype(jnp.bfloat16), earlier, preferred_element_type=jnp.float32)
        slot = lax.broadcasted_iota(jnp.int32, (capacity, rows), 0).astype(jnp.float32)
        return jnp.where(rank == slot, taken, 0.0).astype(jnp.bfloat16)

    def unpacked(picks, value):
        return lax.dot_general(picks, value, (((0,), (0,)), ((), ())), preferred_element_type=jnp.float32)

    def tiles_of(index, body):
        def run(i, carry):
            body(pl.ds(pl.multiple_of(index * cols + i * tile, tile), tile))
            return carry

        lax.fori_loop(0, cols // tile, run, 0)

    def neighbour(upward):
        return exp - 1 if upward else exp + 1

    def is_end(expert, upward):
        return expert == (0 if upward else last)

    def send_result(block, index, upward):
        first = is_end(exp, upward)
        second = is_end(neighbour(upward), upward)

        @pl.when(first)
        def _():
            if index == 0:
                picks = packing(block, exp)
                for slot in range(span):
                    act[slot, block, pl.ds(0, capacity)] = jnp.dot(
                        picks, act[slot, block], preferred_element_type=jnp.float32
                    ).astype(jnp.bfloat16)

            def body(at):
                tok[block, pl.ds(0, capacity), at] = share(block, at, capacity).astype(jnp.bfloat16)

            tiles_of(index, body)
            out_copy(block, index, upward, False, True).start()

        @pl.when(second)
        def _():
            out_copy(block, index, upward, True, True).wait_recv()
            picks = packing(block, neighbour(upward))

            def body(at):
                total = share(block, at) + unpacked(picks, rx[block, pl.ds(0, capacity), at])
                tok[block, :, at] = total.astype(jnp.bfloat16)

            tiles_of(index, body)

        @pl.when(jnp.logical_not(jnp.logical_or(first, second)))
        def _():
            out_copy(block, index, upward, True, False).wait_recv()

            def body(at):
                total = share(block, at) + rx[block, :, at].astype(jnp.float32)
                tok[block, :, at] = total.astype(jnp.bfloat16)

            tiles_of(index, body)

        @pl.when(jnp.logical_not(first))
        def _():
            out_copy(block, index, upward, False, False).start()

    def return_step(step, carry):
        low = exp - (experts - step)
        high = exp + (experts - step)
        for index in range(OUT_PIECES):

            @pl.when(low >= 0)
            def _():
                send_result(jnp.maximum(low, 0), index, False)

            @pl.when(high <= last)
            def _():
                send_result(jnp.minimum(high, last), index, True)

        return carry

    lax.fori_loop(1, experts, return_step, 0)

    def own_body(i, carry):
        at = pl.ds(pl.multiple_of(i * tile, tile), tile)
        acc[:, at] = res_ref[:, at].astype(jnp.float32) + share(exp, at)
        return carry

    lax.fori_loop(0, width // tile, own_body, 0)

    def join(index, upward):
        slot = exp if upward else experts
        second = is_end(neighbour(upward), upward)

        @pl.when(second)
        def _():
            out_copy(exp, index, upward, True, True).wait_recv()
            picks = packing(exp, neighbour(upward))

            def body(at):
                acc[:, at] += unpacked(picks, rx[slot, pl.ds(0, capacity), at])

            tiles_of(index, body)

        @pl.when(jnp.logical_not(jnp.logical_or(second, is_end(exp, upward))))
        def _():
            out_copy(exp, index, upward, True, False).wait_recv()

            def body(at):
                acc[:, at] += rx[slot, :, at].astype(jnp.float32)

            tiles_of(index, body)

    for index in range(OUT_PIECES):
        join(index, True)
        join(index, False)

        def write(at):
            out_ref[:, at] = acc[:, at].astype(jnp.bfloat16)

        tiles_of(index, write)

    def wait_result(block, upward):
        first = is_end(exp, upward)

        @pl.when(first)
        def _():
            for index in range(OUT_PIECES):
                out_copy(block, index, upward, False, True).wait_send()

        @pl.when(jnp.logical_not(first))
        def _():
            for index in range(OUT_PIECES):
                out_copy(block, index, upward, False, False).wait_send()

    def results_sent(block, carry):
        @pl.when(block < exp)
        def _():
            wait_result(block, False)

        @pl.when(block > exp)
        def _():
            wait_result(block, True)

        return carry

    lax.fori_loop(0, experts, results_sent, 0)
    for mat in range(3):
        c_copy(mat, False).wait_send()
        for index in range(W_PIECES[mat]):
            y_copy(mat, index, False).wait_send()
            cy_copy(mat, index, False).wait_send()
            for i in range(groups - 1):
                x_copy(mat, index, i, False).wait_send()
                cx_copy(mat, index, i, False).wait_send()


def shards(residual, norm_gain, router, w_gate, w_up, w_down, expert_ids):
    rows, width = residual.shape
    experts = router.shape[1]
    groups = lax.axis_size("groups")
    span = lax.axis_size("expert") // experts
    assert span == 4
    hid = w_gate.shape[1]
    capacity = 3 * rows * expert_ids.shape[1] // (2 * experts)
    capacity = min(rows, -(-capacity // 16) * 16)
    vmem = pl.BlockSpec(memory_space=pltpu.VMEM)
    anywhere = pl.BlockSpec(memory_space=pl.ANY)
    dma = pltpu.SemaphoreType.DMA
    weight_copies = sum(W_PIECES)
    return pl.pallas_call(
        functools.partial(kernel, groups, experts, span, capacity),
        out_shape=jax.ShapeDtypeStruct((rows, width), jnp.bfloat16),
        in_specs=[vmem, vmem, vmem, vmem, anywhere, anywhere, anywhere],
        out_specs=vmem,
        scratch_shapes=[
            pltpu.VMEM((experts, rows, width), jnp.bfloat16),
            pltpu.VMEM((experts, experts, rows), jnp.float32),
            pltpu.VMEM((span, experts, rows, hid), jnp.bfloat16),
            pltpu.VMEM((experts + 1, rows, width), jnp.bfloat16),
            pltpu.VMEM((rows, width), jnp.float32),
            pltpu.VMEM((span, width, hid), jnp.bfloat16),
            pltpu.VMEM((span, width, hid), jnp.bfloat16),
            pltpu.VMEM((span, hid, width), jnp.bfloat16),
            dma((3,)),
            dma((experts, TOK_PIECES)),
            dma((experts, TOK_PIECES)),
            dma((experts, TOK_PIECES)),
            dma((experts,)),
            dma((experts,)),
            dma((experts,)),
            dma((experts, OUT_PIECES)),
            dma((experts + 1, OUT_PIECES)),
            dma((weight_copies,)),
            dma((weight_copies,)),
            dma((groups - 1, weight_copies)),
            dma((groups - 1, weight_copies)),
            dma((3,)),
            dma((3,)),
            dma((weight_copies,)),
            dma((weight_copies,)),
            dma((groups - 1, weight_copies)),
            dma((groups - 1, weight_copies)),
        ],
        compiler_params=pltpu.CompilerParams(
            collective_id=0, has_side_effects=True, vmem_limit_bytes=67043328
        ),
    )(residual, norm_gain, router.T, expert_ids.T, w_gate, w_up, w_down)


def solution(mesh):
    in_specs = (
        P(("groups", "expert"), None),
        P(),
        P(),
        P(None, "expert"),
        P(None, "expert"),
        P("expert", None),
        P(("groups", "expert"), None),
    )
    out_specs = P(("groups", "expert"), None)
    return jax.shard_map(shards, mesh=mesh, in_specs=in_specs, out_specs=out_specs, check_vma=False)
```

profile of v0, /device:TPU:8, one launch (start us, length us, event | category | flops | bytes accessed | tf_op | source)
XLA Modules:
  0.0 125.7 jit_solution(14643582655347468171)
XLA Ops:
  0.0 123.5 %shard_map.73 = bf16[128,3584]{1,0:T(8,128)(2,1)} custom-call(bf16[128,3584]{1,0:T(8,128)(2,1)} %res_ref.1, f32[3584]{0:T(1024)} %gain_ref.1, bf16[4,3584]{1,0:T(4,128)(2,1)} %bitcast.2, s32[2,128]{1,0:T(2,128)} %bitcast.3, bf16[3584,256]{1,0:T(8,128)(2,1)} %wg_in.1, bf16[3584,256]{1,0:T(8,128)(2,1)} %wu_in.1, bf16[256,3584]{1,0:T(8,128)(2,1)} %wd_in.1), custom_call_target="tpu_custom_call" | custom-call | tf_op jit(solution)/shard_map/pallas_call | solution.py:534
  123.5 2.2 %copy.9 = bf16[128,3584]{1,0:T(8,128)(2,1)} copy(bf16[128,3584]{1,0:T(8,128)(2,1)} %shard_map.73) | data formatting | bytes 1835008
where the time goes:
time: 127 us; the launch traced here: 126 us
  Pallas kernels  124 us (98%)
  local copies, waits for them, and re-layouts  2.16 us (2%)
    pallas_call x1, Pallas kernels, shards(): pl.pallas_call(functools.partial(kernel, groups, experts, span, capacity)...  124 us

commit v1 on v0

v1 whole, which is shorter than its diff:
```python
import functools

import jax
import jax.numpy as jnp
from jax import lax
from jax.experimental import pallas as pl
from jax.experimental.pallas import tpu as pltpu
from jax.sharding import PartitionSpec as P

route_scale = 2.5
norm_eps = 1e-06
LANES = 128
MESH = pl.DeviceIdType.MESH

TOK_PIECES = 8
HEAD = 2
OUT_PIECES = 14
W_PIECES = 8
LAG = 2
SHIFT = 1
AHEAD = 2
OWN_TICK = 4


def kernel(
    groups,
    experts,
    span,
    capacity,
    out_pieces,
    res_ref,
    gain_ref,
    router_ref,
    ids_ref,
    wg_in,
    wu_in,
    wd_in,
    out_ref,
    tok,
    gates,
    act,
    rx,
    acc,
    picked,
    wg,
    wu,
    wd,
    own_sem,
    tok_recv,
    tok_send,
    gate_recv,
    gate_send,
    ret_send,
    ret_recv,
    y_send,
    y_recv,
    x_send,
    x_recv,
    c_send,
    c_recv,
    cy_send,
    cy_recv,
    cx_send,
    cx_recv,
):
    rows, width = res_ref.shape
    grp = lax.axis_index("groups")
    pos = lax.axis_index("expert")
    exp = pos // span
    mem = pos % span
    last = experts - 1
    has_up = exp < last
    has_dn = exp > 0
    base = exp * span
    mem_y = (mem + 2) % 4
    mem_c = mem + 1 - 2 * (mem % 2)
    mem_yc = (mem_c + 2) % 4
    up = {"groups": grp, "expert": jnp.minimum(pos + span, experts * span - 1)}
    dn = {"groups": grp, "expert": jnp.maximum(pos - span, 0)}
    to_y = {"groups": grp, "expert": base + mem_y}
    to_c = {"groups": grp, "expert": base + mem_c}

    def other(i):
        return (grp + 1 + i) % groups

    barrier = pltpu.get_barrier_semaphore()

    def greet(device):
        pl.semaphore_signal(barrier, inc=1, device_id=device, device_id_type=MESH)

    greet(to_y)
    greet(to_c)
    for i in range(groups - 1):
        greet({"groups": other(i), "expert": pos})

    @pl.when(has_up)
    def _():
        greet(up)

    @pl.when(has_dn)
    def _():
        greet(dn)

    peers = 1 + groups + has_up.astype(jnp.int32) + has_dn.astype(jnp.int32)
    pl.semaphore_wait(barrier, peers)

    mats = ((wg_in, wg), (wu_in, wu), (wd_in, wd))
    counts = (W_PIECES, W_PIECES, out_pieces)

    def piece(ref, mat, group, index):
        total = mats[mat][0].shape[mat // 2]
        size = total // groups // counts[mat]
        part = pl.ds(pl.multiple_of((index * groups + group) * size, size), size)
        return ref.at[:, part] if mat == 2 else ref.at[part]

    def number(mat, index):
        return sum(counts[:mat]) + index

    def remote(src, dst, send, recv, device):
        return pltpu.make_async_remote_copy(
            src_ref=src, dst_ref=dst, send_sem=send, recv_sem=recv, device_id=device, device_id_type=MESH
        )

    def y_copy(mat, index, landing):
        at = number(mat, index)
        into = piece(mats[mat][1].at[mem_y if landing else mem], mat, grp, index)
        return remote(piece(mats[mat][0], mat, grp, index), into, y_send.at[at], y_recv.at[at], to_y)

    def x_copy(mat, index, i, landing):
        at = number(mat, index)
        group = (grp + groups - 1 - i) % groups if landing else grp
        ref = piece(mats[mat][1].at[mem_y], mat, group, index)
        return remote(ref, ref, x_send.at[i, at], x_recv.at[i, at], {"groups": other(i), "expert": pos})

    def cy_copy(mat, index, landing):
        at = number(mat, index)
        ref = piece(mats[mat][1].at[mem_yc if landing else mem_y], mat, grp, index)
        return remote(ref, ref, cy_send.at[at], cy_recv.at[at], to_c)

    def cx_copy(mat, index, i, landing):
        at = number(mat, index)
        group = (grp + groups - 1 - i) % groups
        ref = piece(mats[mat][1].at[mem_yc if landing else mem_y], mat, group, index)
        return remote(ref, ref, cx_send.at[i, at], cx_recv.at[i, at], to_c)

    def c_copy(mat, landing):
        slot = mem_c if landing else mem
        return remote(mats[mat][0], mats[mat][1].at[slot], c_send.at[mat], c_recv.at[mat], to_c)

    def loop(count, body):
        def run(i, carry):
            body(i)
            return carry

        lax.fori_loop(0, count, run, 0)

    def start_pair(index):
        for mat in range(2):
            y_copy(mat, index, False).start()

    loop(W_PIECES, start_pair)
    loop(out_pieces, lambda index: y_copy(2, index, False).start())
    own_copies = [pltpu.make_async_copy(mats[i][0], mats[i][1].at[mem], own_sem.at[i]) for i in range(3)]
    for mat in range(3):
        c_copy(mat, False).start()
        own_copies[mat].start()

    step_rows = rows // TOK_PIECES
    tail = TOK_PIECES - HEAD
    ticks = (experts - 2) * TOK_PIECES
    behind = (exp, last - exp)
    onward = (has_up, has_dn)

    def tok_copy(block, index, way):
        ref = tok.at[block, pl.ds(pl.multiple_of(index * step_rows, step_rows), step_rows)]
        return remote(ref, ref, tok_send.at[way, block, index], tok_recv.at[block, index], (up, dn)[way])

    def gate_copy(block, way):
        ref = gates.at[block]
        return remote(ref, ref, gate_send.at[way, block], gate_recv.at[block], (up, dn)[way])

    def norm_rows(index):
        at = pl.ds(pl.multiple_of(index * step_rows, step_rows), step_rows)
        wide = res_ref[at, :].astype(jnp.float32)
        mean = jnp.mean(wide * wide, axis=1, keepdims=True)
        tok[exp, at, :] = (wide * lax.rsqrt(mean + norm_eps) * gain_ref[...].reshape(1, width)).astype(jnp.bfloat16)
        for way in range(2):
            early = jnp.logical_or(index < HEAD, behind[way] == 0)

            @pl.when(jnp.logical_and(onward[way], early))
            def _():
                tok_copy(exp, index, way).start()

    def gate_values():
        logits = lax.dot_general(
            router_ref[...], tok[exp], (((1,), (1,)), ((), ())), preferred_element_type=jnp.float32
        )
        affinity = jax.nn.sigmoid(logits)
        expert = lax.broadcasted_iota(jnp.int32, (experts, rows), 0)
        spread = jnp.zeros((experts, rows), jnp.float32)
        for k in range(ids_ref.shape[0]):
            spread = spread + jnp.where(expert == ids_ref[k : k + 1, :], affinity, 0.0)
        gates[exp] = route_scale * spread / jnp.sum(spread, axis=0, keepdims=True)

    loop(TOK_PIECES, norm_rows)
    gate_values()
    for way in range(2):

        @pl.when(jnp.logical_and(onward[way], behind[way] == 0))
        def _():
            gate_copy(exp, way).start()

    def weight_tick(mat, index):
        y_copy(mat, index, True).wait_recv()
        for i in range(groups - 1):
            x_copy(mat, index, i, False).start()
        cy_copy(mat, index, False).start()

    def weight_late(mat, index):
        for i in range(groups - 1):
            x_copy(mat, index, i, True).wait_recv()
            cx_copy(mat, index, i, False).start()

    def weight_there(mat, index):
        cy_copy(mat, index, True).wait_recv()
        for i in range(groups - 1):
            cx_copy(mat, index, i, True).wait_recv()

    def token_tick(tick, way):
        count = behind[way]
        rest = jnp.maximum(tick - count * HEAD, 0)
        leading = tick < count * HEAD
        dist = jnp.where(leading, tick // HEAD + 1, count - rest // tail)
        dist = jnp.maximum(dist, 1)
        index = jnp.where(leading, tick % HEAD, HEAD + rest % tail)
        block = jnp.maximum(exp - dist, 0) if way == 0 else jnp.minimum(exp + dist, last)
        whole = index == TOK_PIECES - 1

        @pl.when(tick < count * TOK_PIECES)
        def _():
            tok_copy(block, index, way).wait_recv()

            @pl.when(whole)
            def _():
                gate_copy(block, way).wait_recv()

            @pl.when(onward[way])
            def _():
                tok_copy(block, index, way).start()

                @pl.when(whole)
                def _():
                    gate_copy(block, way).start()

                @pl.when(tick == count * TOK_PIECES - 1)
                def _():
                    for own in range(HEAD, TOK_PIECES):
                        tok_copy(exp, own, way).start()
                    gate_copy(exp, way).start()

    def hidden_part(block, slot):
        rows_in = tok[block]
        gate_proj = jnp.dot(rows_in, wg[slot], preferred_element_type=jnp.float32)
        up_proj = jnp.dot(rows_in, wu[slot], preferred_element_type=jnp.float32)
        sublane = lax.broadcasted_iota(jnp.int32, (gates.shape[1], rows), 0)
        row = jnp.sum(jnp.where(sublane == exp, gates[block], 0.0), axis=0, keepdims=True)
        scale = jnp.broadcast_to(row, (LANES, rows)).T[:, :1]
        hidden = gate_proj / (1.0 + jnp.exp(-gate_proj)) * up_proj * scale
        act[slot, block] = hidden.astype(jnp.bfloat16)

    def whole_at(way, dist):
        count = behind[way]
        return count * HEAD + (count - dist + 1) * tail

    def found(tick, way):
        count = behind[way]
        over = tick + 1 - count * HEAD
        dist = count + 1 - over // tail
        there = jnp.logical_and(over > 0, over % tail == 0)
        return jnp.logical_and(there, jnp.logical_and(dist >= 1, dist <= count)), dist

    def first_tick(tick):
        for mat in range(2):

            @pl.when(jnp.logical_and(tick < 2 * W_PIECES, tick % 2 == mat))
            def _():
                weight_tick(mat, tick // 2)

        token_tick(tick, 0)
        token_tick(tick, 1)
        for mat in range(2):
            before = tick - 1

            @pl.when(jnp.logical_and(jnp.logical_and(before >= 0, before < 2 * W_PIECES), tick % 2 != mat))
            def _():
                weight_late(mat, jnp.maximum(before, 0) // 2)

        @pl.when(tick == OWN_TICK)
        def _():
            for mat in range(2):
                own_copies[mat].wait()
                c_copy(mat, True).wait_recv()

        from_dn, dist_dn = found(tick, 0)
        from_up, dist_up = found(tick, 1)
        own = tick == OWN_TICK

        def job(i):
            side = i // 2
            slot = jnp.where(i % 2 == 0, mem, mem_c)
            block = jnp.where(side == 0, exp - dist_dn, jnp.where(side == 1, exp + dist_up, exp))
            valid = jnp.logical_or(
                jnp.logical_and(side == 0, from_dn),
                jnp.logical_or(jnp.logical_and(side == 1, from_up), jnp.logical_and(side == 2, own)),
            )

            @pl.when(valid)
            def _():
                hidden_part(jnp.clip(block, 0, last), slot)

        @pl.when(jnp.logical_or(own, jnp.logical_or(from_dn, from_up)))
        def _():
            loop(6, job)

    total = max(ticks, 2 * W_PIECES, OWN_TICK + 1)
    loop(total, first_tick)
    for index in range(AHEAD):
        weight_tick(2, index)
    if total == 2 * W_PIECES:
        weight_late(1, W_PIECES - 1)
    for index in range(AHEAD - 1):
        weight_late(2, index)

    def pair_there(index):
        for mat in range(2):
            weight_there(mat, index)

    loop(W_PIECES, pair_there)

    def far_job(i):
        dist = last - i // 4
        side = i // 2 % 2
        slot = jnp.where(i % 2 == 0, mem_y, mem_yc)
        valid = False
        for way in range(2):
            full = jnp.logical_and(dist <= behind[way], whole_at(way, dist) <= ticks)
            valid = jnp.logical_or(valid, jnp.logical_and(side == way, full))
        block = jnp.where(side == 0, exp - dist, exp + dist)

        @pl.when(valid)
        def _():
            hidden_part(jnp.clip(block, 0, last), slot)

    loop(4 * last, far_job)
    own_copies[2].wait()
    c_copy(2, True).wait_recv()

    cols = width // out_pieces

    def columns(index):
        return pl.ds(pl.multiple_of(index * cols, cols), cols)

    def out_copy(block, index, way, landing, packed):
        part = columns(index)
        height = pl.ds(0, capacity if packed else rows)
        target = exp if landing else exp - 1
        into = jnp.where(jnp.logical_and(way == 1, block == target), experts, block)
        along = jnp.where(way == 0, jnp.minimum(pos + span, experts * span - 1), jnp.maximum(pos - span, 0))
        return remote(
            tok.at[block, height, part],
            rx.at[into, height, part],
            ret_send.at[block, index],
            ret_recv.at[into, index],
            {"groups": grp, "expert": along},
        )

    def share(block, at, height=rows):
        part = pl.ds(0, height)
        result = jnp.dot(act[0, block, part], wd[0, :, at], preferred_element_type=jnp.float32)
        for slot in range(1, span):
            result = result + jnp.dot(act[slot, block, part], wd[slot, :, at], preferred_element_type=jnp.float32)
        return result

    def packing(block, expert):
        sublane = lax.broadcasted_iota(jnp.int32, (gates.shape[1], rows), 0)
        row = jnp.sum(jnp.where(sublane == expert, gates[block], 0.0), axis=0, keepdims=True)
        taken = jnp.broadcast_to(jnp.where(row != 0.0, 1.0, 0.0), (capacity, rows))
        source = lax.broadcasted_iota(jnp.int32, (rows, rows), 0)
        dest = lax.broadcasted_iota(jnp.int32, (rows, rows), 1)
        earlier = jnp.where(source < dest, 1.0, 0.0).astype(jnp.bfloat16)
        rank = jnp.dot(taken.astype(jnp.bfloat16), earlier, preferred_element_type=jnp.float32)
        slot = lax.broadcasted_iota(jnp.int32, (capacity, rows), 0).astype(jnp.float32)
        return jnp.where(rank == slot, taken, 0.0).astype(jnp.bfloat16)

    def unpacked(way, block, value):
        return lax.dot_general(
            picked[way, block], value, (((0,), (0,)), ((), ())), preferred_element_type=jnp.float32
        )

    def late_rows(block, dist, way):
        for index in range(HEAD, TOK_PIECES):

            @pl.when(jnp.logical_or(dist == 1, index >= TOK_PIECES - HEAD))
            def _():
                tok_copy(block, index, 0).wait_recv()

        gate_copy(block, 0).wait_recv()
        loop(span, lambda slot: hidden_part(block, slot))

    def send_result(block, index, way, dist, count):
        at = columns(index)

        @pl.when(count == 0)
        def _():
            @pl.when(jnp.logical_and(dist <= 2, index == 0))
            def _():
                late_rows(block, dist, way)

            @pl.when(index == 0)
            def _():
                picks = packing(block, exp)

                def pack(slot):
                    act[slot, block, pl.ds(0, capacity)] = jnp.dot(
                        picks, act[slot, block], preferred_element_type=jnp.float32
                    ).astype(jnp.bfloat16)

                loop(span, pack)

            tok[block, pl.ds(0, capacity), at] = share(block, at, capacity).astype(jnp.bfloat16)
            out_copy(block, index, way, False, True).start()

        @pl.when(jnp.logical_and(count > 0, index == 0))
        def _():
            for i in range(TOK_PIECES):
                tok_copy_way(block, i, 1 - way).wait_send()
            gate_copy_way(block, 1 - way).wait_send()

        @pl.when(count == 1)
        def _():
            @pl.when(index == 0)
            def _():
                picked[way, block] = packing(block, jnp.where(way == 0, exp - 1, exp + 1))

            out_copy(block, index, way, True, True).wait_recv()
            result = share(block, at) + unpacked(way, block, rx[block, pl.ds(0, capacity), at])
            tok[block, :, at] = result.astype(jnp.bfloat16)

        @pl.when(count > 1)
        def _():
            out_copy(block, index, way, True, False).wait_recv()
            result = share(block, at) + rx[block, :, at].astype(jnp.float32)
            tok[block, :, at] = result.astype(jnp.bfloat16)

        @pl.when(count > 0)
        def _():
            out_copy(block, index, way, False, False).start()

    def tok_copy_way(block, index, way):
        ref = tok.at[block, pl.ds(pl.multiple_of(index * step_rows, step_rows), step_rows)]
        along = jnp.where(way == 0, up["expert"], dn["expert"])
        device = {"groups": grp, "expert": along}
        return remote(ref, ref, tok_send.at[way, block, index], tok_recv.at[block, index], device)

    def gate_copy_way(block, way):
        ref = gates.at[block]
        along = jnp.where(way == 0, up["expert"], dn["expert"])
        device = {"groups": grp, "expert": along}
        return remote(ref, ref, gate_send.at[way, block], gate_recv.at[block], device)

    def join(index, way, count):
        at = columns(index)
        slot = jnp.where(way == 0, exp, experts)

        @pl.when(count == 1)
        def _():
            @pl.when(index == 0)
            def _():
                picked[way, exp] = packing(exp, jnp.where(way == 0, exp - 1, exp + 1))

            out_copy(exp, index, way, True, True).wait_recv()
            acc[:, at] += unpacked(way, exp, rx[slot, pl.ds(0, capacity), at])

        @pl.when(count > 1)
        def _():
            out_copy(exp, index, way, True, False).wait_recv()
            acc[:, at] += rx[slot, :, at].astype(jnp.float32)

        out_ref[:, at] = acc[:, at].astype(jnp.bfloat16)

    period = out_pieces + SHIFT

    def role(tick, i):
        way = i % 2
        second = i // 2
        count = jnp.where(way == 0, exp, last - exp)
        ahead = last - count
        time = tick - LAG * count
        clock = jnp.maximum(time, 0)
        pair = clock // period
        index = clock % period - SHIFT * second
        far = 2 * pair + second
        dist = ahead - far
        block = jnp.clip(jnp.where(way == 0, exp + dist, exp - dist), 0, last)
        there = jnp.logical_and(time >= 0, jnp.logical_and(index >= 0, index < out_pieces))
        index = jnp.clip(index, 0, out_pieces - 1)

        @pl.when(jnp.logical_and(there, dist > 0))
        def _():
            send_result(block, index, way, dist, count)

        @pl.when(jnp.logical_and(there, jnp.logical_and(dist == 0, count > 0)))
        def _():
            join(index, way, count)

    def second_tick(tick):
        @pl.when(tick + AHEAD < out_pieces)
        def _():
            weight_tick(2, jnp.minimum(tick + AHEAD, out_pieces - 1))

        @pl.when(tick + AHEAD - 1 < out_pieces)
        def _():
            weight_late(2, jnp.minimum(tick + AHEAD - 1, out_pieces - 1))

        @pl.when(tick < out_pieces)
        def _():
            weight_there(2, jnp.minimum(tick, out_pieces - 1))

        loop(4, lambda i: role(tick, i))

        @pl.when(tick == 1)
        def _():
            loop(2, lambda i: hidden_part(exp, jnp.where(i == 0, mem_y, mem_yc)))

        @pl.when(jnp.logical_and(tick >= 1, tick < out_pieces + 1))
        def _():
            at = columns(jnp.clip(tick - 1, 0, out_pieces - 1))
            acc[:, at] = res_ref[:, at].astype(jnp.float32) + share(exp, at)

    loop(-(-experts // 2) * period + LAG * last, second_tick)

    def own_sent(way):
        @pl.when(onward[way])
        def _():
            for index in range(TOK_PIECES):
                tok_copy(exp, index, way).wait_send()
            gate_copy(exp, way).wait_send()

    own_sent(0)
    own_sent(1)

    def results_sent(block):
        def drain(way, packed):
            loop(out_pieces, lambda index: out_copy(block, index, way, False, packed).wait_send())

        for way in range(2):
            passes = block > exp if way == 0 else block < exp

            @pl.when(jnp.logical_and(passes, behind[way] == 0))
            def _():
                drain(way, True)

            @pl.when(jnp.logical_and(passes, behind[way] > 0))
            def _():
                drain(way, False)

    loop(experts, results_sent)

    def weights_sent(mat, index):
        y_copy(mat, index, False).wait_send()
        cy_copy(mat, index, False).wait_send()
        for i in range(groups - 1):
            x_copy(mat, index, i, False).wait_send()
            cx_copy(mat, index, i, False).wait_send()

    for mat in range(3):
        c_copy(mat, False).wait_send()
        loop(counts[mat], functools.partial(weights_sent, mat))


def shards(residual, norm_gain, router, w_gate, w_up, w_down, expert_ids):
    rows, width = residual.shape
    experts = router.shape[1]
    groups = lax.axis_size("groups")
    span = lax.axis_size("expert") // experts
    assert span == 4
    hid = w_gate.shape[1]
    capacity = 3 * rows * expert_ids.shape[1] // (2 * experts)
    capacity = min(rows, -(-capacity // 16) * 16)
    out_pieces = min(OUT_PIECES, width // (groups * LANES))
    vmem = pl.BlockSpec(memory_space=pltpu.VMEM)
    anywhere = pl.BlockSpec(memory_space=pl.ANY)
    dma = pltpu.SemaphoreType.DMA
    weight_copies = 2 * W_PIECES + out_pieces
    return pl.pallas_call(
        functools.partial(kernel, groups, experts, span, capacity, out_pieces),
        out_shape=jax.ShapeDtypeStruct((rows, width), jnp.bfloat16),
        in_specs=[vmem, vmem, vmem, vmem, anywhere, anywhere, anywhere],
        out_specs=vmem,
        scratch_shapes=[
            pltpu.VMEM((experts, rows, width), jnp.bfloat16),
            pltpu.VMEM((experts, experts, rows), jnp.float32),
            pltpu.VMEM((span, experts, rows, hid), jnp.bfloat16),
            pltpu.VMEM((experts + 1, rows, width), jnp.bfloat16),
            pltpu.VMEM((rows, width), jnp.float32),
            pltpu.VMEM((2, experts, capacity, rows), jnp.bfloat16),
            pltpu.VMEM((span, width, hid), jnp.bfloat16),
            pltpu.VMEM((span, width, hid), jnp.bfloat16),
            pltpu.VMEM((span, hid, width), jnp.bfloat16),
            dma((3,)),
            dma((experts, TOK_PIECES)),
            dma((2, experts, TOK_PIECES)),
            dma((experts,)),
            dma((2, experts)),
            dma((experts, out_pieces)),
            dma((experts + 1, out_pieces)),
            dma((weight_copies,)),
            dma((weight_copies,)),
            dma((groups - 1, weight_copies)),
            dma((groups - 1, weight_copies)),
            dma((3,)),
            dma((3,)),
            dma((weight_copies,)),
            dma((weight_copies,)),
            dma((groups - 1, weight_copies)),
            dma((groups - 1, weight_copies)),
        ],
        compiler_params=pltpu.CompilerParams(
            collective_id=0, has_side_effects=True, vmem_limit_bytes=67043328
        ),
    )(residual, norm_gain, router.T, expert_ids.T, w_gate, w_up, w_down)


def solution(mesh):
    in_specs = (
        P(("groups", "expert"), None),
        P(),
        P(),
        P(None, "expert"),
        P(None, "expert"),
        P("expert", None),
        P(("groups", "expert"), None),
    )
    out_specs = P(("groups", "expert"), None)
    return jax.shard_map(shards, mesh=mesh, in_specs=in_specs, out_specs=out_specs, check_vma=False)
```

time: 127 us -> 128 us (level); the launches traced: 126 us -> 128 us
  Pallas kernels: 124 us -> 126 us
    pallas_call x1, Pallas kernels: 124 us -> 126 us  [shards(): pl.pallas_call(functools.partial(kernel, groups, experts, span, capacity,...]
where the time goes in v1:
time: 128 us
  Pallas kernels  126 us (98%)
  local copies, waits for them, and re-layouts  2.16 us (2%)
    pallas_call x1, Pallas kernels, shards(): pl.pallas_call(functools.partial(kernel, groups, experts, span, capacity,...  126 us

profile of v1, /device:TPU:8, one launch (start us, length us, event | category | flops | bytes accessed | tf_op | source)
XLA Modules:
  0.0 128.2 jit_solution(585944761512648881)
XLA Ops:
  0.0 126.0 %shard_map.73 = bf16[128,3584]{1,0:T(8,128)(2,1)} custom-call(bf16[128,3584]{1,0:T(8,128)(2,1)} %res_ref.1, f32[3584]{0:T(1024)} %gain_ref.1, bf16[4,3584]{1,0:T(4,128)(2,1)} %bitcast.2, s32[2,128]{1,0:T(2,128)} %bitcast.3, bf16[3584,256]{1,0:T(8,128)(2,1)} %wg_in.1, bf16[3584,256]{1,0:T(8,128)(2,1)} %wu_in.1, bf16[256,3584]{1,0:T(8,128)(2,1)} %wd_in.1), custom_call_target="tpu_custom_call" | custom-call | tf_op jit(solution)/shard_map/pallas_call | solution.py:595
  126.0 2.2 %copy.9 = bf16[128,3584]{1,0:T(8,128)(2,1)} copy(bf16[128,3584]{1,0:T(8,128)(2,1)} %shard_map.73) | data formatting | bytes 1835008

commit v2 on v1

--- a/solution.py
+++ b/solution.py
@@ -15,10 +15,14 @@
 TOK_PIECES = 8
 HEAD = 2
 OUT_PIECES = 14
-W_PIECES = 8
+W_PIECES = 16
 LAG = 2
-SHIFT = 1
-AHEAD = 2
+SHIFT = 3
+LATE = 2
+AHEAD = 3
+LATE_DOWN = 1
+NEAR = 3
+NEAR_TICKS = 4
 OWN_TICK = 4
 
 
@@ -28,14 +32,19 @@
     span,
     capacity,
     out_pieces,
+    w_pieces,
+    res_in,
+    gain_in,
+    router_in,
+    ids_in,
+    wg_in,
+    wu_in,
+    wd_in,
+    out_ref,
     res_ref,
     gain_ref,
     router_ref,
     ids_ref,
-    wg_in,
-    wu_in,
-    wd_in,
-    out_ref,
     tok,
     gates,
     act,
@@ -45,6 +54,7 @@
     wg,
     wu,
     wd,
+    in_sem,
     own_sem,
     tok_recv,
     tok_send,
@@ -101,11 +111,13 @@
     def _():
         greet(dn)
 
-    peers = 1 + groups + has_up.astype(jnp.int32) + has_dn.astype(jnp.int32)
-    pl.semaphore_wait(barrier, peers)
+    inputs = ((res_in, res_ref), (gain_in, gain_ref), (router_in, router_ref), (ids_in, ids_ref))
+    loads = [pltpu.make_async_copy(*pair, in_sem.at[i]) for i, pair in enumerate(inputs)]
+    for load in loads:
+        load.start()
 
     mats = ((wg_in, wg), (wu_in, wu), (wd_in, wd))
-    counts = (W_PIECES, W_PIECES, out_pieces)
+    counts = (w_pieces, w_pieces, out_pieces)
 
     def piece(ref, mat, group, index):
         total = mats[mat][0].shape[mat // 2]
@@ -124,24 +136,33 @@
     def y_copy(mat, index, landing):
         at = number(mat, index)
         into = piece(mats[mat][1].at[mem_y if landing else mem], mat, grp, index)
-        return remote(piece(mats[mat][0], mat, grp, index), into, y_send.at[at], y_recv.at[at], to_y)
+        return remote(piece(mats[mat][0], mat, grp, index), into, y_send.at[mat], y_recv.at[at], to_y)
 
     def x_copy(mat, index, i, landing):
         at = number(mat, index)
         group = (grp + groups - 1 - i) % groups if landing else grp
         ref = piece(mats[mat][1].at[mem_y], mat, group, index)
-        return remote(ref, ref, x_send.at[i, at], x_recv.at[i, at], {"groups": other(i), "expert": pos})
+        return remote(ref, ref, x_send.at[i, mat], x_recv.at[i, at], {"groups": other(i), "expert": pos})
+
+    def landed(mat, index):
+        return mat if mat < 2 else 2 + index
 
     def cy_copy(mat, index, landing):
-        at = number(mat, index)
+        at = landed(mat, index)
         ref = piece(mats[mat][1].at[mem_yc if landing else mem_y], mat, grp, index)
-        return remote(ref, ref, cy_send.at[at], cy_recv.at[at], to_c)
+        return remote(ref, ref, cy_send.at[mat], cy_recv.at[at], to_c)
 
     def cx_copy(mat, index, i, landing):
-        at = number(mat, index)
+        at = landed(mat, index)
         group = (grp + groups - 1 - i) % groups
         ref = piece(mats[mat][1].at[mem_yc if landing else mem_y], mat, group, index)
-        return remote(ref, ref, cx_send.at[i, at], cx_recv.at[i, at], to_c)
+        return remote(ref, ref, cx_send.at[i, mat], cx_recv.at[i, at], to_c)
+
+    def all_pieces(mat, send, recv, device):
+        ref = mats[mat][1].at[mem_y]
+        part = pl.ds(0, mats[mat][0].shape[mat // 2] // groups)
+        ref = ref.at[:, part] if mat == 2 else ref.at[part]
+        return remote(ref, ref, send, recv, device)
 
     def c_copy(mat, landing):
         slot = mem_c if landing else mem
@@ -158,12 +179,7 @@
         for mat in range(2):
             y_copy(mat, index, False).start()
 
-    loop(W_PIECES, start_pair)
-    loop(out_pieces, lambda index: y_copy(2, index, False).start())
     own_copies = [pltpu.make_async_copy(mats[i][0], mats[i][1].at[mem], own_sem.at[i]) for i in range(3)]
-    for mat in range(3):
-        c_copy(mat, False).start()
-        own_copies[mat].start()
 
     step_rows = rows // TOK_PIECES
     tail = TOK_PIECES - HEAD
@@ -173,7 +189,7 @@
 
     def tok_copy(block, index, way):
         ref = tok.at[block, pl.ds(pl.multiple_of(index * step_rows, step_rows), step_rows)]
-        return remote(ref, ref, tok_send.at[way, block, index], tok_recv.at[block, index], (up, dn)[way])
+        return remote(ref, ref, tok_send.at[way, block], tok_recv.at[block, index], (up, dn)[way])
 
     def gate_copy(block, way):
         ref = gates.at[block]
@@ -183,7 +199,9 @@
         at = pl.ds(pl.multiple_of(index * step_rows, step_rows), step_rows)
         wide = res_ref[at, :].astype(jnp.float32)
         mean = jnp.mean(wide * wide, axis=1, keepdims=True)
-        tok[exp, at, :] = (wide * lax.rsqrt(mean + norm_eps) * gain_ref[...].reshape(1, width)).astype(jnp.bfloat16)
+        tok[exp, at, :] = (wide * lax.rsqrt(mean + norm_eps) * gain_ref[...]).astype(jnp.bfloat16)
+
+    def first_rows(index):
         for way in range(2):
             early = jnp.logical_or(index < HEAD, behind[way] == 0)
 
@@ -202,7 +220,21 @@
             spread = spread + jnp.where(expert == ids_ref[k : k + 1, :], affinity, 0.0)
         gates[exp] = route_scale * spread / jnp.sum(spread, axis=0, keepdims=True)
 
-    loop(TOK_PIECES, norm_rows)
+    peers = 1 + groups + has_up.astype(jnp.int32) + has_dn.astype(jnp.int32)
+    pl.semaphore_wait(barrier, peers)
+    loop(w_pieces, start_pair)
+    for load in loads:
+        load.wait()
+
+    def first_step(index):
+        norm_rows(index)
+        first_rows(index)
+
+    loop(TOK_PIECES, first_step)
+    loop(out_pieces, lambda index: y_copy(2, index, False).start())
+    for mat in range(3):
+        c_copy(mat, False).start()
+        own_copies[mat].start()
     gate_values()
     for way in range(2):
 
@@ -221,10 +253,10 @@
             x_copy(mat, index, i, True).wait_recv()
             cx_copy(mat, index, i, False).start()
 
-    def weight_there(mat, index):
-        cy_copy(mat, index, True).wait_recv()
+    def down_there(index):
+        cy_copy(2, index, True).wait_recv()
         for i in range(groups - 1):
-            cx_copy(mat, index, i, True).wait_recv()
+            cx_copy(2, index, i, True).wait_recv()
 
     def token_tick(tick, way):
         count = behind[way]
@@ -280,20 +312,23 @@
         return jnp.logical_and(there, jnp.logical_and(dist >= 1, dist <= count)), dist
 
     def first_tick(tick):
-        for mat in range(2):
-
-            @pl.when(jnp.logical_and(tick < 2 * W_PIECES, tick % 2 == mat))
-            def _():
-                weight_tick(mat, tick // 2)
+        @pl.when(tick < w_pieces)
+        def _():
+            weight_tick(0, tick)
 
         token_tick(tick, 0)
         token_tick(tick, 1)
-        for mat in range(2):
-            before = tick - 1
-
-            @pl.when(jnp.logical_and(jnp.logical_and(before >= 0, before < 2 * W_PIECES), tick % 2 != mat))
-            def _():
-                weight_late(mat, jnp.maximum(before, 0) // 2)
+
+        @pl.when(tick < w_pieces)
+        def _():
+            weight_tick(1, tick)
+
+        before = tick - LATE
+
+        @pl.when(jnp.logical_and(before >= 0, before < w_pieces))
+        def _():
+            weight_late(0, jnp.maximum(before, 0))
+            weight_late(1, jnp.maximum(before, 0))
 
         @pl.when(tick == OWN_TICK)
         def _():
@@ -322,20 +357,21 @@
         def _():
             loop(6, job)
 
-    total = max(ticks, 2 * W_PIECES, OWN_TICK + 1)
+    total = max(ticks, w_pieces, OWN_TICK + 1)
     loop(total, first_tick)
-    for index in range(AHEAD):
-        weight_tick(2, index)
-    if total == 2 * W_PIECES:
-        weight_late(1, W_PIECES - 1)
-    for index in range(AHEAD - 1):
+    rest = [(mat, before) for before in range(total - LATE, w_pieces) for mat in range(2)]
+    for index in range(max(len(rest), AHEAD - 1)):
+        if index < len(rest):
+            weight_late(*rest[index])
+        if index < AHEAD - 1:
+            weight_tick(2, index)
+    for index in range(LATE_DOWN):
         weight_late(2, index)
-
-    def pair_there(index):
-        for mat in range(2):
-            weight_there(mat, index)
-
-    loop(W_PIECES, pair_there)
+    for mat in range(2):
+        all_pieces(mat, cy_send.at[mat], cy_recv.at[mat], to_c).wait_recv()
+        for i in range(groups - 1):
+            all_pieces(mat, cx_send.at[i, mat], cx_recv.at[i, mat], to_c).wait_recv()
+    weight_tick(2, AHEAD - 1)
 
     def far_job(i):
         dist = last - i // 4
@@ -369,7 +405,7 @@
         return remote(
             tok.at[block, height, part],
             rx.at[into, height, part],
-            ret_send.at[block, index],
+            ret_send.at[block],
             ret_recv.at[into, index],
             {"groups": grp, "expert": along},
         )
@@ -397,7 +433,7 @@
             picked[way, block], value, (((0,), (0,)), ((), ())), preferred_element_type=jnp.float32
         )
 
-    def late_rows(block, dist, way):
+    def late_rows(block, dist):
         for index in range(HEAD, TOK_PIECES):
 
             @pl.when(jnp.logical_or(dist == 1, index >= TOK_PIECES - HEAD))
@@ -405,17 +441,12 @@
                 tok_copy(block, index, 0).wait_recv()
 
         gate_copy(block, 0).wait_recv()
-        loop(span, lambda slot: hidden_part(block, slot))
-
-    def send_result(block, index, way, dist, count):
+
+    def send_result(block, index, way, count):
         at = columns(index)
 
         @pl.when(count == 0)
         def _():
-            @pl.when(jnp.logical_and(dist <= 2, index == 0))
-            def _():
-                late_rows(block, dist, way)
-
             @pl.when(index == 0)
             def _():
                 picks = packing(block, exp)
@@ -432,9 +463,7 @@
 
         @pl.when(jnp.logical_and(count > 0, index == 0))
         def _():
-            for i in range(TOK_PIECES):
-                tok_copy_way(block, i, 1 - way).wait_send()
-            gate_copy_way(block, 1 - way).wait_send()
+            rows_sent(block, 1 - way)
 
         @pl.when(count == 1)
         def _():
@@ -456,17 +485,13 @@
         def _():
             out_copy(block, index, way, False, False).start()
 
-    def tok_copy_way(block, index, way):
-        ref = tok.at[block, pl.ds(pl.multiple_of(index * step_rows, step_rows), step_rows)]
+    def rows_sent(block, way):
         along = jnp.where(way == 0, up["expert"], dn["expert"])
         device = {"groups": grp, "expert": along}
-        return remote(ref, ref, tok_send.at[way, block, index], tok_recv.at[block, index], device)
-
-    def gate_copy_way(block, way):
+        ref = tok.at[block]
+        remote(ref, ref, tok_send.at[way, block], tok_recv.at[block, 0], device).wait_send()
         ref = gates.at[block]
-        along = jnp.where(way == 0, up["expert"], dn["expert"])
-        device = {"groups": grp, "expert": along}
-        return remote(ref, ref, gate_send.at[way, block], gate_recv.at[block], device)
+        remote(ref, ref, gate_send.at[way, block], gate_recv.at[block], device).wait_send()
 
     def join(index, way, count):
         at = columns(index)
@@ -489,13 +514,62 @@
         out_ref[:, at] = acc[:, at].astype(jnp.bfloat16)
 
     period = out_pieces + SHIFT
+
+    def after(far):
+        return far // 2 * period + far % 2 * SHIFT + out_pieces
+
+    defer = after(last - 1)
+
+    def delay(count):
+        return jnp.where(count == last, defer, LAG * count)
+
+    near = LAG + after(last - 2) - NEAR_TICKS
+
+    def until(count):
+        end = delay(count) + after(jnp.where(count > 0, last - count, last - 1))
+        return jnp.where(count == 1, near - (-out_pieces // NEAR), end)
+
+    at_end = jnp.logical_or(exp == 0, exp == last)
+    own_start = jnp.where(at_end, out_pieces, OWN_TICK - 1)
+
+    def tick_job(tick):
+        block, rest, due = exp, 1, tick == own_start
+        for dist in (1, 2):
+            first = (last - dist) // 2 * period + (last - dist) % 2 * SHIFT - 2
+            away = jnp.where(exp == 0, dist, last - dist)
+            begins = jnp.logical_and(at_end, tick == first)
+
+            @pl.when(begins)
+            def _():
+                late_rows(away, dist)
+
+            now = jnp.logical_and(at_end, jnp.logical_or(tick == first, tick == first + 1))
+            block, rest = jnp.where(now, away, block), jnp.where(now, tick - first, rest)
+            due = jnp.logical_or(due, now)
+
+        def part(i):
+            own = jnp.where(i == 0, mem, mem_c)
+            hidden_part(block, jnp.where(rest == 0, own, (own + 2) % 4))
+
+        @pl.when(due)
+        def _():
+            loop(2, part)
+
+    def near_joins(tick):
+        for way in range(2):
+            for i in range(NEAR):
+                index = (tick - near) * NEAR + i
+
+                @pl.when(jnp.logical_and(behind[way] == 1, jnp.logical_and(index >= 0, index < out_pieces)))
+                def _():
+                    join(jnp.clip(index, 0, out_pieces - 1), way, behind[way])
 
     def role(tick, i):
         way = i % 2
         second = i // 2
         count = jnp.where(way == 0, exp, last - exp)
         ahead = last - count
-        time = tick - LAG * count
+        time = tick - delay(count)
         clock = jnp.maximum(time, 0)
         pair = clock // period
         index = clock % period - SHIFT * second
@@ -507,75 +581,64 @@
 
         @pl.when(jnp.logical_and(there, dist > 0))
         def _():
-            send_result(block, index, way, dist, count)
-
-        @pl.when(jnp.logical_and(there, jnp.logical_and(dist == 0, count > 0)))
+            send_result(block, index, way, count)
+
+        @pl.when(jnp.logical_and(there, jnp.logical_and(dist == 0, count > 1)))
         def _():
             join(index, way, count)
 
     def second_tick(tick):
+        @pl.when(tick < out_pieces)
+        def _():
+            down_there(jnp.minimum(tick, out_pieces - 1))
+
+        loop(4, lambda i: role(tick, i))
+
         @pl.when(tick + AHEAD < out_pieces)
         def _():
             weight_tick(2, jnp.minimum(tick + AHEAD, out_pieces - 1))
 
-        @pl.when(tick + AHEAD - 1 < out_pieces)
-        def _():
-            weight_late(2, jnp.minimum(tick + AHEAD - 1, out_pieces - 1))
-
-        @pl.when(tick < out_pieces)
-        def _():
-            weight_there(2, jnp.minimum(tick, out_pieces - 1))
-
-        loop(4, lambda i: role(tick, i))
-
-        @pl.when(tick == 1)
-        def _():
-            loop(2, lambda i: hidden_part(exp, jnp.where(i == 0, mem_y, mem_yc)))
-
-        @pl.when(jnp.logical_and(tick >= 1, tick < out_pieces + 1))
-        def _():
-            at = columns(jnp.clip(tick - 1, 0, out_pieces - 1))
+        @pl.when(tick + LATE_DOWN < out_pieces)
+        def _():
+            weight_late(2, jnp.minimum(tick + LATE_DOWN, out_pieces - 1))
+
+        tick_job(tick)
+        turn = tick - own_start
+
+        @pl.when(jnp.logical_and(turn >= 0, turn < out_pieces))
+        def _():
+            at = columns(jnp.clip(turn, 0, out_pieces - 1))
             acc[:, at] = res_ref[:, at].astype(jnp.float32) + share(exp, at)
 
-    loop(-(-experts // 2) * period + LAG * last, second_tick)
-
-    def own_sent(way):
+        near_joins(tick)
+
+    loop(jnp.maximum(until(behind[0]), until(behind[1])), second_tick)
+
+    for way in range(2):
+
         @pl.when(onward[way])
         def _():
-            for index in range(TOK_PIECES):
-                tok_copy(exp, index, way).wait_send()
-            gate_copy(exp, way).wait_send()
-
-    own_sent(0)
-    own_sent(1)
+            rows_sent(exp, way)
 
     def results_sent(block):
-        def drain(way, packed):
-            loop(out_pieces, lambda index: out_copy(block, index, way, False, packed).wait_send())
-
         for way in range(2):
             passes = block > exp if way == 0 else block < exp
-
-            @pl.when(jnp.logical_and(passes, behind[way] == 0))
-            def _():
-                drain(way, True)
-
-            @pl.when(jnp.logical_and(passes, behind[way] > 0))
-            def _():
-                drain(way, False)
+            for packed in (True, False):
+
+                @pl.when(jnp.logical_and(passes, (behind[way] == 0) == packed))
+                def _():
+                    ref = tok.at[block, pl.ds(0, capacity if packed else rows)]
+                    remote(ref, ref, ret_send.at[block], ret_recv.at[block, 0], (up, dn)[way]).wait_send()
 
     loop(experts, results_sent)
-
-    def weights_sent(mat, index):
-        y_copy(mat, index, False).wait_send()
-        cy_copy(mat, index, False).wait_send()
-        for i in range(groups - 1):
-            x_copy(mat, index, i, False).wait_send()
-            cx_copy(mat, index, i, False).wait_send()
-
     for mat in range(3):
         c_copy(mat, False).wait_send()
-        loop(counts[mat], functools.partial(weights_sent, mat))
+        all_pieces(mat, y_send.at[mat], y_recv.at[mat], to_y).wait_send()
+        all_pieces(mat, cy_send.at[mat], cy_recv.at[mat], to_c).wait_send()
+        for i in range(groups - 1):
+            device = {"groups": other(i), "expert": pos}
+            all_pieces(mat, x_send.at[i, mat], x_recv.at[i, mat], device).wait_send()
+            all_pieces(mat, cx_send.at[i, mat], cx_recv.at[i, mat], to_c).wait_send()
 
 
 def shards(residual, norm_gain, router, w_gate, w_up, w_down, expert_ids):
@@ -588,16 +651,23 @@
     capacity = 3 * rows * expert_ids.shape[1] // (2 * experts)
     capacity = min(rows, -(-capacity // 16) * 16)
     out_pieces = min(OUT_PIECES, width // (groups * LANES))
+    w_pieces = W_PIECES
+    while width // groups // w_pieces % 16:
+        w_pieces //= 2
     vmem = pl.BlockSpec(memory_space=pltpu.VMEM)
     anywhere = pl.BlockSpec(memory_space=pl.ANY)
     dma = pltpu.SemaphoreType.DMA
-    weight_copies = 2 * W_PIECES + out_pieces
+    weight_copies = 2 * w_pieces + out_pieces
     return pl.pallas_call(
-        functools.partial(kernel, groups, experts, span, capacity, out_pieces),
+        functools.partial(kernel, groups, experts, span, capacity, out_pieces, w_pieces),
         out_shape=jax.ShapeDtypeStruct((rows, width), jnp.bfloat16),
-        in_specs=[vmem, vmem, vmem, vmem, anywhere, anywhere, anywhere],
+        in_specs=[anywhere] * 7,
         out_specs=vmem,
         scratch_shapes=[
+            pltpu.VMEM((rows, width), residual.dtype),
+            pltpu.VMEM((1, width), norm_gain.dtype),
+            pltpu.VMEM((experts, width), router.dtype),
+            pltpu.VMEM(expert_ids.shape[::-1], expert_ids.dtype),
             pltpu.VMEM((experts, rows, width), jnp.bfloat16),
             pltpu.VMEM((experts, experts, rows), jnp.float32),
             pltpu.VMEM((span, experts, rows, hid), jnp.bfloat16),
@@ -607,28 +677,29 @@
             pltpu.VMEM((span, width, hid), jnp.bfloat16),
             pltpu.VMEM((span, width, hid), jnp.bfloat16),
             pltpu.VMEM((span, hid, width), jnp.bfloat16),
+            dma((4,)),
             dma((3,)),
             dma((experts, TOK_PIECES)),
-            dma((2, experts, TOK_PIECES)),
+            dma((2, experts)),
             dma((experts,)),
             dma((2, experts)),
-            dma((experts, out_pieces)),
+            dma((experts,)),
             dma((experts + 1, out_pieces)),
+            dma((3,)),
             dma((weight_copies,)),
-            dma((weight_copies,)),
-            dma((groups - 1, weight_copies)),
+            dma((groups - 1, 3)),
             dma((groups - 1, weight_copies)),
             dma((3,)),
             dma((3,)),
-            dma((weight_copies,)),
-            dma((weight_copies,)),
-            dma((groups - 1, weight_copies)),
-            dma((groups - 1, weight_copies)),
+            dma((3,)),
+            dma((2 + out_pieces,)),
+            dma((groups - 1, 3)),
+            dma((groups - 1, 2 + out_pieces)),
         ],
         compiler_params=pltpu.CompilerParams(
             collective_id=0, has_side_effects=True, vmem_limit_bytes=67043328
         ),
-    )(residual, norm_gain, router.T, expert_ids.T, w_gate, w_up, w_down)
+    )(residual, norm_gain[None], router.T, expert_ids.T, w_gate, w_up, w_down)
 
 
 def solution(mesh):

time: 128 us -> 109 us (0.85)
  Pallas kernels: 126 us -> 105 us
  local copies, waits for them, and re-layouts: 2.16 us -> 3.49 us
    pallas_call x1, Pallas kernels: 126 us -> 105 us  [shards(): pl.pallas_call(functools.partial(kernel, groups, experts, span, capacity,...]
    broadcast_in_dim x0 -> x1, local copies, waits for them, and re-layouts: none -> 1.33 us  [shards(): norm_gain[None]]
where the time goes in v2:
time: 109 us; the launch traced here: 108 us
  Pallas kernels  105 us (96%)
  local copies, waits for them, and re-layouts  3.49 us (3%)
    pallas_call x1, Pallas kernels, shards(): pl.pallas_call(functools.partial(kernel, groups, experts, span, capacity,...  105 us

profile of v2, /device:TPU:8, one launch (start us, length us, event | category | flops | bytes accessed | tf_op | source)
XLA Modules:
  0.0 108.2 jit_solution(13034978160747798643)
XLA Ops:
  0.0 1.3 %broadcast_in_dim.3.gain_in = f32[1,3584]{1,0:T(1,128)} reshape(f32[3584]{0:T(1024)} %param.8) | data formatting | bytes 28672 | tf_op jit(solution)/shard_map/broadcast_in_dim | solution.py:702
  1.3 104.7 %shard_map.73 = bf16[128,3584]{1,0:T(8,128)(2,1)} custom-call(bf16[128,3584]{1,0:T(8,128)(2,1)} %res_in.1, f32[1,3584]{1,0:T(1,128)} %broadcast_in_dim.3.gain_in, bf16[4,3584]{1,0:T(4,128)(2,1)} %bitcast.2, s32[2,128]{1,0:T(2,128)} %bitcast.3, bf16[3584,256]{1,0:T(8,128)(2,1)} %wg_in.1, bf16[3584,256]{1,0:T(8,128)(2,1)} %wu_in.1, bf16[256,3584]{1,0:T(8,128)(2,1)} %wd_in.1), custom_call_target="tpu_custom_call" | custom-call | tf_op jit(solution)/shard_map/pallas_call | solution.py:661
  106.0 2.2 %copy.9 = bf16[128,3584]{1,0:T(8,128)(2,1)} copy(bf16[128,3584]{1,0:T(8,128)(2,1)} %shard_map.73) | data formatting | bytes 1835008

commit v3 on v2

--- a/solution.py
+++ b/solution.py
@@ -17,13 +17,15 @@
 OUT_PIECES = 14
 W_PIECES = 16
 LAG = 2
-SHIFT = 3
+SHIFT = 4
 LATE = 2
 AHEAD = 3
-LATE_DOWN = 1
-NEAR = 3
-NEAR_TICKS = 4
-OWN_TICK = 4
+RELAYS = 3
+JOINS = 3
+JOIN_TICKS = 4
+JOIN_LAG = 2
+OWN_TICK = 5
+OWN_START = 4
 
 
 def kernel(
@@ -56,12 +58,11 @@
     wd,
     in_sem,
     own_sem,
-    tok_recv,
+    land,
     tok_send,
     gate_recv,
     gate_send,
     ret_send,
-    ret_recv,
     y_send,
     y_recv,
     x_send,
@@ -135,11 +136,11 @@
 
     def y_copy(mat, index, landing):
         at = number(mat, index)
-        into = piece(mats[mat][1].at[mem_y if landing else mem], mat, grp, index)
-        return remote(piece(mats[mat][0], mat, grp, index), into, y_send.at[mat], y_recv.at[at], to_y)
+        ref = piece(mats[mat][1].at[mem_y if landing else mem], mat, grp, index)
+        return remote(ref, ref, y_send.at[mat], y_recv.at[at], to_y)
 
     def x_copy(mat, index, i, landing):
-        at = number(mat, index)
+        at = index if mat < 2 else w_pieces + index
         group = (grp + groups - 1 - i) % groups if landing else grp
         ref = piece(mats[mat][1].at[mem_y], mat, group, index)
         return remote(ref, ref, x_send.at[i, mat], x_recv.at[i, at], {"groups": other(i), "expert": pos})
@@ -165,8 +166,8 @@
         return remote(ref, ref, send, recv, device)
 
     def c_copy(mat, landing):
-        slot = mem_c if landing else mem
-        return remote(mats[mat][0], mats[mat][1].at[slot], c_send.at[mat], c_recv.at[mat], to_c)
+        ref = mats[mat][1].at[mem_c if landing else mem]
+        return remote(ref, ref, c_send.at[mat], c_recv.at[mat], to_c)
 
     def loop(count, body):
         def run(i, carry):
@@ -180,6 +181,8 @@
             y_copy(mat, index, False).start()
 
     own_copies = [pltpu.make_async_copy(mats[i][0], mats[i][1].at[mem], own_sem.at[i]) for i in range(3)]
+    for mat in range(3):
+        own_copies[mat].start()
 
     step_rows = rows // TOK_PIECES
     tail = TOK_PIECES - HEAD
@@ -189,7 +192,7 @@
 
     def tok_copy(block, index, way):
         ref = tok.at[block, pl.ds(pl.multiple_of(index * step_rows, step_rows), step_rows)]
-        return remote(ref, ref, tok_send.at[way, block], tok_recv.at[block, index], (up, dn)[way])
+        return remote(ref, ref, tok_send.at[way, block], land.at[block, index], (up, dn)[way])
 
     def gate_copy(block, way):
         ref = gates.at[block]
@@ -199,7 +202,7 @@
         at = pl.ds(pl.multiple_of(index * step_rows, step_rows), step_rows)
         wide = res_ref[at, :].astype(jnp.float32)
         mean = jnp.mean(wide * wide, axis=1, keepdims=True)
-        tok[exp, at, :] = (wide * lax.rsqrt(mean + norm_eps) * gain_ref[...]).astype(jnp.bfloat16)
+        tok[exp, at, :] = (wide * lax.rsqrt(mean + norm_eps) * gain_ref[...].reshape(1, width)).astype(jnp.bfloat16)
 
     def first_rows(index):
         for way in range(2):
@@ -222,6 +225,8 @@
 
     peers = 1 + groups + has_up.astype(jnp.int32) + has_dn.astype(jnp.int32)
     pl.semaphore_wait(barrier, peers)
+    for mat in range(2):
+        own_copies[mat].wait()
     loop(w_pieces, start_pair)
     for load in loads:
         load.wait()
@@ -231,10 +236,10 @@
         first_rows(index)
 
     loop(TOK_PIECES, first_step)
+    own_copies[2].wait()
     loop(out_pieces, lambda index: y_copy(2, index, False).start())
     for mat in range(3):
         c_copy(mat, False).start()
-        own_copies[mat].start()
     gate_values()
     for way in range(2):
 
@@ -248,17 +253,26 @@
             x_copy(mat, index, i, False).start()
         cy_copy(mat, index, False).start()
 
-    def weight_late(mat, index):
+    def weight_late(index):
         for i in range(groups - 1):
-            x_copy(mat, index, i, True).wait_recv()
-            cx_copy(mat, index, i, False).start()
+            x_copy(2, index, i, True).wait_recv()
+            cx_copy(2, index, i, False).start()
+
+    def pair_late(index):
+        both = wg.at[mem_y].at[pl.ds(0, 2 * (width // groups // w_pieces))]
+        for i in range(groups - 1):
+            device = {"groups": other(i), "expert": pos}
+            remote(both, both, x_send.at[i, 0], x_recv.at[i, index], device).wait_recv()
+            for mat in range(2):
+                cx_copy(mat, index, i, False).start()
 
     def down_there(index):
         cy_copy(2, index, True).wait_recv()
         for i in range(groups - 1):
             cx_copy(2, index, i, True).wait_recv()
 
-    def token_tick(tick, way):
+    def token_tick(step, way):
+        tick = jnp.maximum(step, 0)
         count = behind[way]
         rest = jnp.maximum(tick - count * HEAD, 0)
         leading = tick < count * HEAD
@@ -268,7 +282,7 @@
         block = jnp.maximum(exp - dist, 0) if way == 0 else jnp.minimum(exp + dist, last)
         whole = index == TOK_PIECES - 1
 
-        @pl.when(tick < count * TOK_PIECES)
+        @pl.when(jnp.logical_and(step >= 0, tick < count * TOK_PIECES))
         def _():
             tok_copy(block, index, way).wait_recv()
 
@@ -316,8 +330,12 @@
         def _():
             weight_tick(0, tick)
 
-        token_tick(tick, 0)
-        token_tick(tick, 1)
+        @pl.when(tick == w_pieces)
+        def _():
+            weight_tick(2, 0)
+
+        token_tick(tick - 1, 0)
+        token_tick(tick - 1, 1)
 
         @pl.when(tick < w_pieces)
         def _():
@@ -327,17 +345,15 @@
 
         @pl.when(jnp.logical_and(before >= 0, before < w_pieces))
         def _():
-            weight_late(0, jnp.maximum(before, 0))
-            weight_late(1, jnp.maximum(before, 0))
+            pair_late(jnp.maximum(before, 0))
 
         @pl.when(tick == OWN_TICK)
         def _():
             for mat in range(2):
-                own_copies[mat].wait()
                 c_copy(mat, True).wait_recv()
 
-        from_dn, dist_dn = found(tick, 0)
-        from_up, dist_up = found(tick, 1)
+        from_dn, dist_dn = found(tick - 1, 0)
+        from_up, dist_up = found(tick - 1, 1)
         own = tick == OWN_TICK
 
         def job(i):
@@ -357,26 +373,18 @@
         def _():
             loop(6, job)
 
-    total = max(ticks, w_pieces, OWN_TICK + 1)
+    total = max(ticks, w_pieces) + 1
     loop(total, first_tick)
-    rest = [(mat, before) for before in range(total - LATE, w_pieces) for mat in range(2)]
+    rest = list(range(total - LATE, w_pieces))
     for index in range(max(len(rest), AHEAD - 1)):
         if index < len(rest):
-            weight_late(*rest[index])
-        if index < AHEAD - 1:
+            pair_late(rest[index])
+        if 0 < index < AHEAD - 1:
             weight_tick(2, index)
-    for index in range(LATE_DOWN):
-        weight_late(2, index)
-    for mat in range(2):
-        all_pieces(mat, cy_send.at[mat], cy_recv.at[mat], to_c).wait_recv()
-        for i in range(groups - 1):
-            all_pieces(mat, cx_send.at[i, mat], cx_recv.at[i, mat], to_c).wait_recv()
-    weight_tick(2, AHEAD - 1)
-
-    def far_job(i):
-        dist = last - i // 4
-        side = i // 2 % 2
-        slot = jnp.where(i % 2 == 0, mem_y, mem_yc)
+
+    def far_job(first, i):
+        dist = last - i // 2
+        side = i % 2
         valid = False
         for way in range(2):
             full = jnp.logical_and(dist <= behind[way], whole_at(way, dist) <= ticks)
@@ -385,10 +393,31 @@
 
         @pl.when(valid)
         def _():
-            hidden_part(jnp.clip(block, 0, last), slot)
-
-    loop(4 * last, far_job)
-    own_copies[2].wait()
+            hidden_part(jnp.clip(block, 0, last), mem_y if first else mem_yc)
+
+    def far_first(i):
+        far_job(True, i)
+
+        @pl.when(i == 1)
+        def _():
+            weight_late(0)
+
+    def far_second(i):
+        far_job(False, i)
+        order = i // 2
+
+        @pl.when(jnp.logical_and(i % 2 == 1, order < RELAYS))
+        def _():
+            weight_tick(2, AHEAD - 1 + jnp.minimum(order, RELAYS - 1))
+
+    loop(2 * last, far_first)
+    for mat in range(2):
+        all_pieces(mat, cy_send.at[mat], cy_recv.at[mat], to_c).wait_recv()
+        for i in range(groups - 1):
+            all_pieces(mat, cx_send.at[i, mat], cx_recv.at[i, mat], to_c).wait_recv()
+    loop(2 * last, far_second)
+    weight_late(1)
+    sent_on = AHEAD - 1 + RELAYS
     c_copy(2, True).wait_recv()
 
     cols = width // out_pieces
@@ -406,7 +435,7 @@
             tok.at[block, height, part],
             rx.at[into, height, part],
             ret_send.at[block],
-            ret_recv.at[into, index],
+            land.at[into, index],
             {"groups": grp, "expert": along},
         )
 
@@ -489,7 +518,7 @@
         along = jnp.where(way == 0, up["expert"], dn["expert"])
         device = {"groups": grp, "expert": along}
         ref = tok.at[block]
-        remote(ref, ref, tok_send.at[way, block], tok_recv.at[block, 0], device).wait_send()
+        remote(ref, ref, tok_send.at[way, block], land.at[block, 0], device).wait_send()
         ref = gates.at[block]
         remote(ref, ref, gate_send.at[way, block], gate_recv.at[block], device).wait_send()
 
@@ -518,24 +547,27 @@
     def after(far):
         return far // 2 * period + far % 2 * SHIFT + out_pieces
 
-    defer = after(last - 1)
-
-    def delay(count):
-        return jnp.where(count == last, defer, LAG * count)
-
-    near = LAG + after(last - 2) - NEAR_TICKS
+    def joins(count):
+        far = last - count
+        start = LAG * count + far // 2 * period + far % 2 * SHIFT + JOIN_LAG
+        start = jnp.where(count == last, after(last - 1), start)
+        start = jnp.where(count == 1, LAG + after(last - 2) - JOIN_TICKS, start)
+        rate = jnp.where(count == 1, JOINS, jnp.where(count == last, 2, 1))
+        return start, rate
 
     def until(count):
-        end = delay(count) + after(jnp.where(count > 0, last - count, last - 1))
-        return jnp.where(count == 1, near - (-out_pieces // NEAR), end)
+        start, rate = joins(count)
+        send_end = LAG * count + after(jnp.maximum(last - count - 1, 0))
+        join_end = start + (out_pieces + rate - 1) // jnp.maximum(rate, 1)
+        return jnp.maximum(jnp.where(count < last, send_end, 0), jnp.where(count > 0, join_end, 0))
 
     at_end = jnp.logical_or(exp == 0, exp == last)
-    own_start = jnp.where(at_end, out_pieces, OWN_TICK - 1)
+    own_start = jnp.where(at_end, 2 * (period // 2 + 1), OWN_START)
 
     def tick_job(tick):
-        block, rest, due = exp, 1, tick == own_start
+        block, slot, due = exp, jnp.where(tick == own_start, mem_y, mem_yc), tick // 2 == own_start // 2
         for dist in (1, 2):
-            first = (last - dist) // 2 * period + (last - dist) % 2 * SHIFT - 2
+            first = (last - dist) // 2 * period + (last - dist) % 2 * SHIFT - SHIFT
             away = jnp.where(exp == 0, dist, last - dist)
             begins = jnp.logical_and(at_end, tick == first)
 
@@ -543,33 +575,36 @@
             def _():
                 late_rows(away, dist)
 
-            now = jnp.logical_and(at_end, jnp.logical_or(tick == first, tick == first + 1))
-            block, rest = jnp.where(now, away, block), jnp.where(now, tick - first, rest)
+            turn = tick - first
+            now = jnp.logical_and(at_end, jnp.logical_and(turn >= 0, turn < span))
+            block, slot = jnp.where(now, away, block), jnp.where(now, (mem + turn) % span, slot)
             due = jnp.logical_or(due, now)
 
-        def part(i):
-            own = jnp.where(i == 0, mem, mem_c)
-            hidden_part(block, jnp.where(rest == 0, own, (own + 2) % 4))
-
         @pl.when(due)
         def _():
-            loop(2, part)
-
-    def near_joins(tick):
-        for way in range(2):
-            for i in range(NEAR):
-                index = (tick - near) * NEAR + i
-
-                @pl.when(jnp.logical_and(behind[way] == 1, jnp.logical_and(index >= 0, index < out_pieces)))
-                def _():
-                    join(jnp.clip(index, 0, out_pieces - 1), way, behind[way])
+            hidden_part(block, slot)
+
+    def join_tick(tick, way):
+        count = behind[way]
+        start, rate = joins(count)
+
+        def one(i):
+            index = (tick - start) * rate + i
+
+            @pl.when(jnp.logical_and(index >= 0, index < out_pieces))
+            def _():
+                join(jnp.clip(index, 0, out_pieces - 1), way, count)
+
+        @pl.when(jnp.logical_and(count > 0, tick >= start))
+        def _():
+            loop(rate, one)
 
     def role(tick, i):
         way = i % 2
         second = i // 2
         count = jnp.where(way == 0, exp, last - exp)
         ahead = last - count
-        time = tick - delay(count)
+        time = tick - LAG * count
         clock = jnp.maximum(time, 0)
         pair = clock // period
         index = clock % period - SHIFT * second
@@ -583,10 +618,6 @@
         def _():
             send_result(block, index, way, count)
 
-        @pl.when(jnp.logical_and(there, jnp.logical_and(dist == 0, count > 1)))
-        def _():
-            join(index, way, count)
-
     def second_tick(tick):
         @pl.when(tick < out_pieces)
         def _():
@@ -594,23 +625,24 @@
 
         loop(4, lambda i: role(tick, i))
 
-        @pl.when(tick + AHEAD < out_pieces)
-        def _():
-            weight_tick(2, jnp.minimum(tick + AHEAD, out_pieces - 1))
-
-        @pl.when(tick + LATE_DOWN < out_pieces)
-        def _():
-            weight_late(2, jnp.minimum(tick + LATE_DOWN, out_pieces - 1))
+        @pl.when(tick + sent_on < out_pieces)
+        def _():
+            weight_tick(2, jnp.minimum(tick + sent_on, out_pieces - 1))
+
+        @pl.when(tick + 2 < out_pieces)
+        def _():
+            weight_late(jnp.minimum(tick + 2, out_pieces - 1))
 
         tick_job(tick)
-        turn = tick - own_start
+        turn = tick - own_start - 1
 
         @pl.when(jnp.logical_and(turn >= 0, turn < out_pieces))
         def _():
             at = columns(jnp.clip(turn, 0, out_pieces - 1))
             acc[:, at] = res_ref[:, at].astype(jnp.float32) + share(exp, at)
 
-        near_joins(tick)
+        join_tick(tick, 0)
+        join_tick(tick, 1)
 
     loop(jnp.maximum(until(behind[0]), until(behind[1])), second_tick)
 
@@ -628,7 +660,7 @@
                 @pl.when(jnp.logical_and(passes, (behind[way] == 0) == packed))
                 def _():
                     ref = tok.at[block, pl.ds(0, capacity if packed else rows)]
-                    remote(ref, ref, ret_send.at[block], ret_recv.at[block, 0], (up, dn)[way]).wait_send()
+                    remote(ref, ref, ret_send.at[block], land.at[block, 0], (up, dn)[way]).wait_send()
 
     loop(experts, results_sent)
     for mat in range(3):
@@ -660,12 +692,12 @@
     weight_copies = 2 * w_pieces + out_pieces
     return pl.pallas_call(
         functools.partial(kernel, groups, experts, span, capacity, out_pieces, w_pieces),
-        out_shape=jax.ShapeDtypeStruct((rows, width), jnp.bfloat16),
+        out_shape=pltpu.VMEM((rows, width), jnp.bfloat16),
         in_specs=[anywhere] * 7,
         out_specs=vmem,
         scratch_shapes=[
             pltpu.VMEM((rows, width), residual.dtype),
-            pltpu.VMEM((1, width), norm_gain.dtype),
+            pltpu.VMEM((width,), norm_gain.dtype),
             pltpu.VMEM((experts, width), router.dtype),
             pltpu.VMEM(expert_ids.shape[::-1], expert_ids.dtype),
             pltpu.VMEM((experts, rows, width), jnp.bfloat16),
@@ -679,16 +711,15 @@
             pltpu.VMEM((span, hid, width), jnp.bfloat16),
             dma((4,)),
             dma((3,)),
-            dma((experts, TOK_PIECES)),
+            dma((experts + 1, max(TOK_PIECES, out_pieces))),
             dma((2, experts)),
             dma((experts,)),
             dma((2, experts)),
             dma((experts,)),
-            dma((experts + 1, out_pieces)),
             dma((3,)),
             dma((weight_copies,)),
             dma((groups - 1, 3)),
-            dma((groups - 1, weight_copies)),
+            dma((groups - 1, w_pieces + out_pieces)),
             dma((3,)),
             dma((3,)),
             dma((3,)),
@@ -697,9 +728,9 @@
             dma((groups - 1, 2 + out_pieces)),
         ],
         compiler_params=pltpu.CompilerParams(
-            collective_id=0, has_side_effects=True, vmem_limit_bytes=67043328
+            collective_id=0, has_side_effects=True, vmem_limit_bytes=67043328 - 2 * rows * width
         ),
-    )(residual, norm_gain[None], router.T, expert_ids.T, w_gate, w_up, w_down)
+    )(residual, norm_gain, router.T, expert_ids.T, w_gate, w_up, w_down)
 
 
 def solution(mesh):

time: 109 us -> 106 us (0.972)
  local copies, waits for them, and re-layouts: 3.49 us -> 0.93 us
    broadcast_in_dim x1 -> x0, local copies, waits for them, and re-layouts: 1.33 us -> none  [shards(): norm_gain[None]]
    unnamed x1, local copies, waits for them, and re-layouts: 2.16 us -> 0.93 us
where the time goes in v3:
time: 106 us; the launch traced here: 105 us
  Pallas kernels  104 us (98%)
    pallas_call x1, Pallas kernels, shards(): pl.pallas_call(functools.partial(kernel, groups, experts, span, capacity,...  104 us

profile of v3, /device:TPU:8, one launch (start us, length us, event | category | flops | bytes accessed | tf_op | source)
XLA Modules:
  0.0 105.0 jit_solution(16963469371417353416)
XLA Ops:
  0.0 104.1 %shard_map.73 = bf16[128,3584]{1,0:T(8,128)(2,1)S(1)} custom-call(bf16[128,3584]{1,0:T(8,128)(2,1)} %res_in.1, f32[3584]{0:T(1024)} %gain_in.1, bf16[4,3584]{1,0:T(4,128)(2,1)} %bitcast.2, s32[2,128]{1,0:T(2,128)} %bitcast.3, bf16[3584,256]{1,0:T(8,128)(2,1)} %wg_in.1, bf16[3584,256]{1,0:T(8,128)(2,1)} %wu_in.1, bf16[256,3584]{1,0:T(8,128)(2,1)} %wd_in.1), custom_call_target="tpu_custom_call" | custom-call | tf_op jit(solution)/shard_map/pallas_call | solution.py:693
  104.1 0.9 copy.9

commit v4 on v3

--- a/solution.py
+++ b/solution.py
@@ -20,7 +20,7 @@
 SHIFT = 4
 LATE = 2
 AHEAD = 3
-RELAYS = 3
+RELAYS = 1
 JOINS = 3
 JOIN_TICKS = 4
 JOIN_LAG = 2
@@ -373,14 +373,47 @@
         def _():
             loop(6, job)
 
+    def packing(block, expert):
+        sublane = lax.broadcasted_iota(jnp.int32, (gates.shape[1], rows), 0)
+        row = jnp.sum(jnp.where(sublane == expert, gates[block], 0.0), axis=0, keepdims=True)
+        taken = jnp.broadcast_to(jnp.where(row != 0.0, 1.0, 0.0), (capacity, rows))
+        source = lax.broadcasted_iota(jnp.int32, (rows, rows), 0)
+        dest = lax.broadcasted_iota(jnp.int32, (rows, rows), 1)
+        earlier = jnp.where(source < dest, 1.0, 0.0).astype(jnp.bfloat16)
+        rank = jnp.dot(taken.astype(jnp.bfloat16), earlier, preferred_element_type=jnp.float32)
+        slot = lax.broadcasted_iota(jnp.int32, (capacity, rows), 0).astype(jnp.float32)
+        return jnp.where(rank == slot, taken, 0.0).astype(jnp.bfloat16)
+
+    at_end = jnp.logical_or(exp == 0, exp == last)
+
+    end_way = jnp.where(exp == 0, 0, 1)
+
+    def pick(block):
+        picked[end_way, block] = packing(block, exp)
+
+    def pack(block, slot):
+        act[slot, block, pl.ds(0, capacity)] = jnp.dot(
+            picked[end_way, block], act[slot, block], preferred_element_type=jnp.float32
+        ).astype(jnp.bfloat16)
+
+    def pick_far(i):
+        block = jnp.where(exp == 0, last - i, i)
+        pick(block)
+        pack(block, mem)
+        pack(block, mem_c)
+
     total = max(ticks, w_pieces) + 1
     loop(total, first_tick)
     rest = list(range(total - LATE, w_pieces))
-    for index in range(max(len(rest), AHEAD - 1)):
-        if index < len(rest):
-            pair_late(rest[index])
-        if 0 < index < AHEAD - 1:
-            weight_tick(2, index)
+    weight_tick(2, 1)
+
+    @pl.when(at_end)
+    def _():
+        loop(last - 2, pick_far)
+
+    for index in rest:
+        pair_late(index)
+    weight_tick(2, 2)
 
     def far_job(first, i):
         dist = last - i // 2
@@ -393,7 +426,12 @@
 
         @pl.when(valid)
         def _():
-            hidden_part(jnp.clip(block, 0, last), mem_y if first else mem_yc)
+            slot = mem_y if first else mem_yc
+            hidden_part(jnp.clip(block, 0, last), slot)
+
+            @pl.when(at_end)
+            def _():
+                pack(jnp.clip(block, 0, last), slot)
 
     def far_first(i):
         far_job(True, i)
@@ -408,7 +446,7 @@
 
         @pl.when(jnp.logical_and(i % 2 == 1, order < RELAYS))
         def _():
-            weight_tick(2, AHEAD - 1 + jnp.minimum(order, RELAYS - 1))
+            weight_tick(2, AHEAD + jnp.minimum(order, RELAYS - 1))
 
     loop(2 * last, far_first)
     for mat in range(2):
@@ -417,7 +455,7 @@
             all_pieces(mat, cx_send.at[i, mat], cx_recv.at[i, mat], to_c).wait_recv()
     loop(2 * last, far_second)
     weight_late(1)
-    sent_on = AHEAD - 1 + RELAYS
+    sent_on = AHEAD + RELAYS
     c_copy(2, True).wait_recv()
 
     cols = width // out_pieces
@@ -446,17 +484,6 @@
             result = result + jnp.dot(act[slot, block, part], wd[slot, :, at], preferred_element_type=jnp.float32)
         return result
 
-    def packing(block, expert):
-        sublane = lax.broadcasted_iota(jnp.int32, (gates.shape[1], rows), 0)
-        row = jnp.sum(jnp.where(sublane == expert, gates[block], 0.0), axis=0, keepdims=True)
-        taken = jnp.broadcast_to(jnp.where(row != 0.0, 1.0, 0.0), (capacity, rows))
-        source = lax.broadcasted_iota(jnp.int32, (rows, rows), 0)
-        dest = lax.broadcasted_iota(jnp.int32, (rows, rows), 1)
-        earlier = jnp.where(source < dest, 1.0, 0.0).astype(jnp.bfloat16)
-        rank = jnp.dot(taken.astype(jnp.bfloat16), earlier, preferred_element_type=jnp.float32)
-        slot = lax.broadcasted_iota(jnp.int32, (capacity, rows), 0).astype(jnp.float32)
-        return jnp.where(rank == slot, taken, 0.0).astype(jnp.bfloat16)
-
     def unpacked(way, block, value):
         return lax.dot_general(
             picked[way, block], value, (((0,), (0,)), ((), ())), preferred_element_type=jnp.float32
@@ -470,23 +497,13 @@
                 tok_copy(block, index, 0).wait_recv()
 
         gate_copy(block, 0).wait_recv()
+        pick(block)
 
     def send_result(block, index, way, count):
         at = columns(index)
 
         @pl.when(count == 0)
         def _():
-            @pl.when(index == 0)
-            def _():
-                picks = packing(block, exp)
-
-                def pack(slot):
-                    act[slot, block, pl.ds(0, capacity)] = jnp.dot(
-                        picks, act[slot, block], preferred_element_type=jnp.float32
-                    ).astype(jnp.bfloat16)
-
-                loop(span, pack)
-
             tok[block, pl.ds(0, capacity), at] = share(block, at, capacity).astype(jnp.bfloat16)
             out_copy(block, index, way, False, True).start()
 
@@ -561,7 +578,6 @@
         join_end = start + (out_pieces + rate - 1) // jnp.maximum(rate, 1)
         return jnp.maximum(jnp.where(count < last, send_end, 0), jnp.where(count > 0, join_end, 0))
 
-    at_end = jnp.logical_or(exp == 0, exp == last)
     own_start = jnp.where(at_end, 2 * (period // 2 + 1), OWN_START)
 
     def tick_job(tick):
@@ -583,6 +599,10 @@
         @pl.when(due)
         def _():
             hidden_part(block, slot)
+
+            @pl.when(block != exp)
+            def _():
+                pack(block, slot)
 
     def join_tick(tick, way):
         count = behind[way]
@@ -624,6 +644,7 @@
             down_there(jnp.minimum(tick, out_pieces - 1))
 
         loop(4, lambda i: role(tick, i))
+        tick_job(tick)
 
         @pl.when(tick + sent_on < out_pieces)
         def _():
@@ -633,7 +654,6 @@
         def _():
             weight_late(jnp.minimum(tick + 2, out_pieces - 1))
 
-        tick_job(tick)
         turn = tick - own_start - 1
 
         @pl.when(jnp.logical_and(turn >= 0, turn < out_pieces))

time: 106 us -> 105 us (level)
  no operation moved by 1% of the time
where the time goes in v4:
time: 105 us
  Pallas kernels  104 us (99%)
    pallas_call x1, Pallas kernels, shards(): pl.pallas_call(functools.partial(kernel, groups, experts, span, capacity,...  104 us

profile of v4, /device:TPU:8, one launch (start us, length us, event | category | flops | bytes accessed | tf_op | source)
XLA Modules:
  0.0 104.5 jit_solution(18318826443463199482)
XLA Ops:
  0.0 103.6 %shard_map.73 = bf16[128,3584]{1,0:T(8,128)(2,1)S(1)} custom-call(bf16[128,3584]{1,0:T(8,128)(2,1)} %res_in.1, f32[3584]{0:T(1024)} %gain_in.1, bf16[4,3584]{1,0:T(4,128)(2,1)} %bitcast.2, s32[2,128]{1,0:T(2,128)} %bitcast.3, bf16[3584,256]{1,0:T(8,128)(2,1)} %wg_in.1, bf16[3584,256]{1,0:T(8,128)(2,1)} %wu_in.1, bf16[256,3584]{1,0:T(8,128)(2,1)} %wd_in.1), custom_call_target="tpu_custom_call" | custom-call | tf_op jit(solution)/shard_map/pallas_call | solution.py:713
  103.6 0.9 copy.9

commit v5 on v4

--- a/solution.py
+++ b/solution.py
@@ -22,7 +22,7 @@
 AHEAD = 3
 RELAYS = 1
 JOINS = 3
-JOIN_TICKS = 4
+JOIN_TICKS = 3
 JOIN_LAG = 2
 OWN_TICK = 5
 OWN_START = 4

time: 105 us -> 104 us (level)
  no operation moved by 1% of the time
where the time goes in v5:
time: 104 us
  Pallas kernels  103 us (99%)
    pallas_call x1, Pallas kernels, shards(): pl.pallas_call(functools.partial(kernel, groups, experts, span, capacity,...  103 us

profile of v5, /device:TPU:8, one launch (start us, length us, event | category | flops | bytes accessed | tf_op | source)
XLA Modules:
  0.0 104.2 jit_solution(12801149453873498700)
XLA Ops:
  0.0 103.3 %shard_map.73 = bf16[128,3584]{1,0:T(8,128)(2,1)S(1)} custom-call(bf16[128,3584]{1,0:T(8,128)(2,1)} %res_in.1, f32[3584]{0:T(1024)} %gain_in.1, bf16[4,3584]{1,0:T(4,128)(2,1)} %bitcast.2, s32[2,128]{1,0:T(2,128)} %bitcast.3, bf16[3584,256]{1,0:T(8,128)(2,1)} %wg_in.1, bf16[3584,256]{1,0:T(8,128)(2,1)} %wu_in.1, bf16[256,3584]{1,0:T(8,128)(2,1)} %wd_in.1), custom_call_target="tpu_custom_call" | custom-call | tf_op jit(solution)/shard_map/pallas_call | solution.py:713
  103.3 0.9 copy.9
